TPU v7x, 32 devices: a whole 2x2x4 slice. The times are simulated.
32 devices in a mesh: gx: 4 (over z), gy: 2 (over core), gz: 4 (over y, x).
Axes of the slice: x: 2, y: 2, z: 4, core: 2. Of those that a mesh axis runs over, the one named last changes fastest.
Arguments:
- tokens: bfloat16 [16384, 768], P(('gx', 'gy', 'gz')), may hold values from -6 to 6
- segment_ids: int32 [8, 2048], P(('gx', 'gy')), may hold values from 0 to 15, never falling along the last dimension, each value on 1 to 1024 neighbouring positions
- valid_mask: int32 [8, 2048], P(('gx', 'gy')), may hold values from 0 to 1, as said below
- cotangent: bfloat16 [16384, 768], P(('gx', 'gy', 'gz')), may hold values from -6 to 6
- teacher: bfloat16 [16384, 768], P(('gx', 'gy', 'gz')), may hold values from -6 to 6
- w_query: bfloat16 [768, 768], P('gy', 'gz'), may hold values from -0.21875 to 0.21875
- b_query: bfloat16 [768], P('gz'), may hold values from -3 to 3
- w_key: bfloat16 [768, 768], P('gy', 'gz'), may hold values from -0.21875 to 0.21875
- w_value: bfloat16 [768, 768], P('gy', 'gz'), may hold values from -0.21875 to 0.21875
- b_value: bfloat16 [768], P('gz'), may hold values from -0.5 to 0.5
- w_out: bfloat16 [768, 768], P('gz', 'gy'), may hold values from -1.75 to 1.75
- b_out: bfloat16 [768], replicated, may hold values from -1.1953125 to 1.1953125
- norm1_gain: bfloat16 [768], replicated, may hold values from 0.5 to 1.5
- norm1_bias: bfloat16 [768], replicated, may hold values from -1.1953125 to 1.1953125
- w_up: bfloat16 [768, 3072], P('gy', 'gz'), may hold values from -0.21875 to 0.21875
- b_up: bfloat16 [3072], P('gz'), may hold values from -3 to 3
- w_down: bfloat16 [3072, 768], P('gz', 'gy'), may hold values from -0.109375 to 0.109375
- b_down: bfloat16 [768], replicated, may hold values from -1.1953125 to 1.1953125
- norm2_gain: bfloat16 [768], replicated, may hold values from 0.5 to 1.5
- norm2_bias: bfloat16 [768], replicated, may hold values from -1.1953125 to 1.1953125
Outputs:
- output: bfloat16 [16384, 768], P(('gx', 'gy', 'gz'))
- mean_loss: float32 [], replicated
- d_tokens: bfloat16 [16384, 768], P(('gx', 'gy', 'gz'))
- d_w_query: float32 [768, 768], P('gy', 'gz')
- d_b_query: float32 [768], P('gz')
- d_w_key: float32 [768, 768], P('gy', 'gz')
- d_w_value: float32 [768, 768], P('gy', 'gz')
- d_b_value: float32 [768], P('gz')
- d_w_out: float32 [768, 768], P('gz', 'gy')
- d_b_out: float32 [768], replicated
- d_norm1_gain: float32 [768], replicated
- d_norm1_bias: float32 [768], replicated
- d_w_up: float32 [768, 3072], P('gy', 'gz')
- d_b_up: float32 [3072], P('gz')
- d_w_down: float32 [3072, 768], P('gz', 'gy')
- d_b_down: float32 [768], replicated
- d_norm2_gain: float32 [768], replicated
- d_norm2_bias: float32 [768], replicated
Inputs may be any that keep to these rules, and one draw needn't show every extreme that they name: `segment_ids`: within a sequence the ids never fall, and each id that occurs forms one run of 1 to 1024 positions. `valid_mask`: in each sequence the valid tokens are a leading run of 512 positions or more, padding after it.
All inputs are finite; a program needn't handle non-finite values.
Results may differ from a plain program's by a relative error of at most 0.02.
Values may be sent and summed in bfloat16 or wider, within the bound.
No kernel may reach another device: no remote copies, remote signals or barrier semaphores. Data moves between devices by JAX's collectives and lax.ppermute only.
A program may use at most 128 MiB of HBM per device.

v0:
```python
import math

import jax
import jax.numpy as jnp
from jax import lax
from jax.sharding import PartitionSpec as P

HEAD = 64


MASKED = -1e30
EPSILON = 1e-05


def gather_rows(tensor):
    return lax.all_gather(tensor, "gz", axis=0, tiled=True)


def sum_rows(term_fn, row_count):
    return lax.psum_scatter(
        term_fn(jnp.int32(0), lax.axis_size("gz") * row_count).astype(jnp.bfloat16),
        "gz",
        scatter_dimension=0,
        tiled=True,
    ).astype(jnp.float32)


def norm_forward(resid, gain, shift):
    average = jnp.mean(resid, -1, keepdims=True)
    centered = resid - average
    inv_std = lax.rsqrt(jnp.mean(centered * centered, -1, keepdims=True) + EPSILON)
    normed = centered * inv_std
    return (normed * gain + shift, normed, inv_std)


def norm_backward(upstream, normed, inv_std, gain):
    d_gain = jnp.sum(upstream * normed, 0)
    d_shift = jnp.sum(upstream, 0)
    scaled = upstream * gain
    d_resid = inv_std * (
        scaled
        - jnp.mean(scaled, -1, keepdims=True)
        - normed * jnp.mean(scaled * normed, -1, keepdims=True)
    )
    return (d_resid, d_gain, d_shift)


def gelu_parts(preact):
    normal_cdf = 0.5 * (1.0 + lax.erf(preact * (1.0 / math.sqrt(2.0))))
    slope = normal_cdf + preact * jnp.exp(-0.5 * preact * preact) * (1.0 / math.sqrt(2.0 * math.pi))
    return (preact * normal_cdf, slope)


def allowed_block(seg_row, valid_row, first_row, block_rows):
    query_pos = first_row + jnp.arange(block_rows, dtype=jnp.int32)
    key_pos = jnp.arange(seg_row.shape[0], dtype=jnp.int32)
    query_seg = lax.dynamic_slice_in_dim(seg_row, first_row, block_rows)
    return (query_seg[:, None] == seg_row[None, :]) & (
        (valid_row[None, :] == 1) | (query_pos[:, None] == key_pos[None, :])
    )


def attention_forward(queries, key_rows, value_rows, seg_row, valid_row, block_rows):
    length, col_width = queries.shape
    head_count = col_width // HEAD
    score_scale = HEAD ** (-0.5)

    def one_block(block_index):
        first_row = block_index * block_rows
        allowed = allowed_block(seg_row, valid_row, first_row, block_rows)
        query_block = lax.dynamic_slice_in_dim(queries, first_row, block_rows)
        outputs = []
        log_parts = []
        for head_index in range(head_count):
            columns = slice(head_index * HEAD, (head_index + 1) * HEAD)
            scores = (
                jnp.einsum(
                    "qd,kd->qk",
                    query_block[:, columns],
                    key_rows[:, columns],
                    preferred_element_type=jnp.float32,
                )
                * score_scale
            )
            scores = jnp.where(allowed, scores, MASKED)
            row_max = jnp.max(scores, -1, keepdims=True)
            weights = jnp.exp(scores - row_max)
            exp_total = jnp.sum(weights, -1, keepdims=True)
            probs_low = (weights / exp_total).astype(jnp.bfloat16)
            outputs.append(
                jnp.dot(probs_low, value_rows[:, columns], preferred_element_type=jnp.float32)
            )
            log_parts.append((row_max + jnp.log(exp_total))[:, 0])
        return (jnp.concatenate(outputs, 1), jnp.stack(log_parts, 1))

    outputs, log_sums = lax.map(one_block, jnp.arange(length // block_rows, dtype=jnp.int32))
    return (outputs.reshape(length, col_width), log_sums.reshape(length, head_count))


def attention_backward(
    queries, key_rows, value_rows, d_attended, log_sums, seg_row, valid_row, block_rows
):
    length, col_width = queries.shape
    head_count = col_width // HEAD
    score_scale = HEAD ** (-0.5)

    def one_block(carried, block_index):
        d_key_sum, d_value_sum = carried
        first_row = block_index * block_rows
        allowed = allowed_block(seg_row, valid_row, first_row, block_rows)
        query_block = lax.dynamic_slice_in_dim(queries, first_row, block_rows)
        grad_block = lax.dynamic_slice_in_dim(d_attended, first_row, block_rows)
        log_block = lax.dynamic_slice_in_dim(log_sums, first_row, block_rows)
        query_parts = []
        key_parts = []
        value_parts = []
        for head_index in range(head_count):
            columns = slice(head_index * HEAD, (head_index + 1) * HEAD)
            scores = (
                jnp.einsum(
                    "qd,kd->qk",
                    query_block[:, columns],
                    key_rows[:, columns],
                    preferred_element_type=jnp.float32,
                )
                * score_scale
            )
            scores = jnp.where(allowed, scores, MASKED)
            probs = jnp.exp(scores - log_block[:, head_index : head_index + 1])
            d_probs = jnp.einsum(
                "qd,kd->qk",
                grad_block[:, columns],
                value_rows[:, columns],
                preferred_element_type=jnp.float32,
            )
            d_scores = (probs * (d_probs - jnp.sum(probs * d_probs, -1, keepdims=True))).astype(
                jnp.bfloat16
            )
            query_parts.append(
                jnp.dot(d_scores, key_rows[:, columns], preferred_element_type=jnp.float32)
                * score_scale
            )
            key_parts.append(
                jnp.einsum(
                    "qk,qd->kd",
                    d_scores,
                    query_block[:, columns],
                    preferred_element_type=jnp.float32,
                )
                * score_scale
            )
            value_parts.append(
                jnp.einsum(
                    "qk,qd->kd",
                    probs.astype(jnp.bfloat16),
                    grad_block[:, columns],
                    preferred_element_type=jnp.float32,
                )
            )
        d_key_sum = d_key_sum + jnp.concatenate(key_parts, 1)
        d_value_sum = d_value_sum + jnp.concatenate(value_parts, 1)
        return ((d_key_sum, d_value_sum), jnp.concatenate(query_parts, 1))

    zero_rows = jnp.zeros((length, col_width), jnp.float32)
    (d_key_sum, d_value_sum), d_query_blocks = lax.scan(
        one_block, (zero_rows, zero_rows), jnp.arange(length // block_rows, dtype=jnp.int32)
    )
    return (d_query_blocks.reshape(length, col_width), d_key_sum, d_value_sum)


def shards(
    tokens,
    segment_ids,
    valid_mask,
    cotangent,
    teacher,
    w_query,
    b_query,
    w_key,
    w_value,
    b_value,
    w_out,
    b_out,
    norm1_gain,
    norm1_bias,
    w_up,
    b_up,
    w_down,
    b_down,
    norm2_gain,
    norm2_bias,
):
    row_count = tokens.shape[0]
    group_rows = row_count * lax.axis_size("gz")
    block_rows = min(512, group_rows)
    own_first = lax.axis_index("gz") * row_count
    seg_row = segment_ids[0]
    valid_row = valid_mask[0]
    own_valid = lax.dynamic_slice_in_dim(valid_row, own_first, row_count).astype(jnp.float32)[
        :, None
    ]
    query_cols, key_cols, value_cols, up_cols = (
        lax.all_gather(w_query, "gy", axis=0, tiled=True),
        lax.all_gather(w_key, "gy", axis=0, tiled=True),
        lax.all_gather(w_value, "gy", axis=0, tiled=True),
        lax.all_gather(w_up, "gy", axis=0, tiled=True),
    )
    out_rows, down_rows = (
        lax.all_gather(w_out, "gy", axis=1, tiled=True),
        lax.all_gather(w_down, "gy", axis=1, tiled=True),
    )
    col_width = query_cols.shape[1]
    qkv_weight = jnp.concatenate([query_cols, key_cols, value_cols], 1)
    qkv_bias = jnp.concatenate(
        [
            b_query.astype(jnp.float32),
            jnp.zeros((col_width,), jnp.float32),
            b_value.astype(jnp.float32),
        ]
    )
    tokens_all = gather_rows(tokens)
    projected = (
        jnp.dot(tokens_all, qkv_weight, preferred_element_type=jnp.float32) + qkv_bias
    ).astype(jnp.bfloat16)
    queries = projected[:, :col_width]
    key_rows = projected[:, col_width : 2 * col_width]
    value_rows = projected[:, 2 * col_width :]
    attended, log_sums = attention_forward(
        queries, key_rows, value_rows, seg_row, valid_row, block_rows
    )
    attended = attended.astype(jnp.bfloat16)

    def out_term(first_row, span_rows):
        return jnp.dot(
            lax.dynamic_slice_in_dim(attended, first_row, span_rows),
            out_rows,
            preferred_element_type=jnp.float32,
        )

    mixed_rows = sum_rows(out_term, row_count) + b_out.astype(jnp.float32)
    resid1 = tokens.astype(jnp.float32) + mixed_rows
    hidden, normed1, inv_std1 = norm_forward(
        resid1, norm1_gain.astype(jnp.float32), norm1_bias.astype(jnp.float32)
    )
    hidden_low = hidden.astype(jnp.bfloat16)
    hidden_all = gather_rows(hidden_low)
    preact = jnp.dot(hidden_all, up_cols, preferred_element_type=jnp.float32) + b_up.astype(
        jnp.float32
    )
    activated, slope = gelu_parts(preact)
    activated = activated.astype(jnp.bfloat16)

    def down_term(first_row, span_rows):
        return jnp.dot(
            lax.dynamic_slice_in_dim(activated, first_row, span_rows),
            down_rows,
            preferred_element_type=jnp.float32,
        )

    branch = sum_rows(down_term, row_count)
    resid2 = hidden + (branch + b_down.astype(jnp.float32))
    norm2_gain_f = norm2_gain.astype(jnp.float32)
    output_full, normed2, inv_std2 = norm_forward(
        resid2, norm2_gain_f, norm2_bias.astype(jnp.float32)
    )
    mismatch = output_full - teacher.astype(jnp.float32)
    error_part = jnp.sum(own_valid * mismatch * mismatch)
    count_part = jnp.sum(own_valid)
    d_output = cotangent.astype(jnp.float32) + own_valid * mismatch
    d_resid2, d_norm2_gain, d_norm2_bias = norm_backward(d_output, normed2, inv_std2, norm2_gain_f)
    d_branch = d_resid2.astype(jnp.bfloat16)
    d_b_down = jnp.sum(d_branch, 0, dtype=jnp.float32)
    d_branch_all = gather_rows(d_branch)
    d_act = jnp.einsum("lm,fm->lf", d_branch_all, down_rows, preferred_element_type=jnp.float32)
    d_down = jnp.einsum("lf,lm->fm", activated, d_branch_all, preferred_element_type=jnp.float32)
    d_pre = (d_act * slope).astype(jnp.bfloat16)
    d_bias_up = jnp.sum(d_pre, 0, dtype=jnp.float32)
    d_up = jnp.einsum("lm,lf->mf", hidden_all, d_pre, preferred_element_type=jnp.float32)

    def back_term(first_row, span_rows):
        return jnp.einsum(
            "lf,mf->lm",
            lax.dynamic_slice_in_dim(d_pre, first_row, span_rows),
            up_cols,
            preferred_element_type=jnp.float32,
        )

    d_hidden = d_resid2 + sum_rows(back_term, row_count)
    d_resid1, d_norm1_gain, d_norm1_bias = norm_backward(
        d_hidden, normed1, inv_std1, norm1_gain.astype(jnp.float32)
    )
    d_mixed = d_resid1.astype(jnp.bfloat16)
    d_b_out = jnp.sum(d_mixed, 0, dtype=jnp.float32)
    d_mixed_all = gather_rows(d_mixed)
    d_attended = jnp.einsum(
        "lm,cm->lc", d_mixed_all, out_rows, preferred_element_type=jnp.float32
    ).astype(jnp.bfloat16)
    d_out_w = jnp.einsum("lc,lm->cm", attended, d_mixed_all, preferred_element_type=jnp.float32)
    d_query_rows, d_key_rows, d_value_rows = attention_backward(
        queries, key_rows, value_rows, d_attended, log_sums, seg_row, valid_row, block_rows
    )
    d_projected = jnp.concatenate([d_query_rows, d_key_rows, d_value_rows], 1).astype(jnp.bfloat16)
    d_qkv_w = jnp.einsum("lm,lc->mc", tokens_all, d_projected, preferred_element_type=jnp.float32)
    d_bias_qkv = jnp.sum(d_projected, 0, dtype=jnp.float32)

    def input_term(first_row, span_rows):
        return jnp.einsum(
            "lc,mc->lm",
            lax.dynamic_slice_in_dim(d_projected, first_row, span_rows),
            qkv_weight,
            preferred_element_type=jnp.float32,
        )

    d_tokens = d_resid1 + sum_rows(input_term, row_count)
    grad_query, grad_key, grad_value, grad_up = (
        lax.psum_scatter(
            d_qkv_w[:, :col_width].astype(jnp.bfloat16), "gy", scatter_dimension=0, tiled=True
        ).astype(jnp.float32),
        lax.psum_scatter(
            d_qkv_w[:, col_width : 2 * col_width].astype(jnp.bfloat16),
            "gy",
            scatter_dimension=0,
            tiled=True,
        ).astype(jnp.float32),
        lax.psum_scatter(
            d_qkv_w[:, 2 * col_width :].astype(jnp.bfloat16), "gy", scatter_dimension=0, tiled=True
        ).astype(jnp.float32),
        lax.psum_scatter(d_up.astype(jnp.bfloat16), "gy", scatter_dimension=0, tiled=True).astype(
            jnp.float32
        ),
    )
    grad_out, grad_down = (
        lax.psum_scatter(
            d_out_w.astype(jnp.bfloat16), "gy", scatter_dimension=1, tiled=True
        ).astype(jnp.float32),
        lax.psum_scatter(d_down.astype(jnp.bfloat16), "gy", scatter_dimension=1, tiled=True).astype(
            jnp.float32
        ),
    )
    grad_query, grad_key, grad_value, grad_up, grad_out, grad_down = (
        lax.psum(grad_query.astype(jnp.bfloat16), "gx").astype(jnp.float32),
        lax.psum(grad_key.astype(jnp.bfloat16), "gx").astype(jnp.float32),
        lax.psum(grad_value.astype(jnp.bfloat16), "gx").astype(jnp.float32),
        lax.psum(grad_up.astype(jnp.bfloat16), "gx").astype(jnp.float32),
        lax.psum(grad_out.astype(jnp.bfloat16), "gx").astype(jnp.float32),
        lax.psum(grad_down.astype(jnp.bfloat16), "gx").astype(jnp.float32),
    )
    grad_b_query, grad_b_value, grad_b_up = lax.psum(
        (d_bias_qkv[:col_width], d_bias_qkv[2 * col_width :], d_bias_up), ("gx", "gy")
    )
    (
        grad_gain1,
        grad_shift1,
        grad_gain2,
        grad_shift2,
        grad_b_out,
        grad_b_down,
        error_sum,
        count_sum,
    ) = lax.psum(
        (
            d_norm1_gain,
            d_norm1_bias,
            d_norm2_gain,
            d_norm2_bias,
            d_b_out,
            d_b_down,
            error_part,
            count_part,
        ),
        ("gx", "gy", "gz"),
    )
    mean_loss = error_sum / (count_sum * tokens.shape[1])
    return (
        output_full.astype(jnp.bfloat16),
        mean_loss,
        d_tokens.astype(jnp.bfloat16),
        grad_query,
        grad_b_query,
        grad_key,
        grad_value,
        grad_b_value,
        grad_out,
        grad_b_out,
        grad_gain1,
        grad_shift1,
        grad_up,
        grad_b_up,
        grad_down,
        grad_b_down,
        grad_gain2,
        grad_shift2,
    )


def solution(mesh):
    placed = (
        P(("gx", "gy", "gz"), None),
        P(("gx", "gy"), None),
        P(("gx", "gy"), None),
        P(("gx", "gy", "gz"), None),
        P(("gx", "gy", "gz"), None),
        P("gy", "gz"),
        P("gz"),
        P("gy", "gz"),
        P("gy", "gz"),
        P("gz"),
        P("gz", "gy"),
        P(),
        P(),
        P(),
        P("gy", "gz"),
        P("gz"),
        P("gz", "gy"),
        P(),
        P(),
        P(),
    )
    return jax.shard_map(
        shards,
        mesh=mesh,
        in_specs=placed,
        out_specs=(
            P(("gx", "gy", "gz"), None),
            P(),
            P(("gx", "gy", "gz"), None),
            P("gy", "gz"),
            P("gz"),
            P("gy", "gz"),
            P("gy", "gz"),
            P("gz"),
            P("gz", "gy"),
            P(),
            P(),
            P(),
            P("gy", "gz"),
            P("gz"),
            P("gz", "gy"),
            P(),
            P(),
            P(),
        ),
        check_vma=False,
    )
```

profile of v0, /device:TPU:0, one launch (start us, length us, event | category | flops | bytes accessed | tf_op | source)
XLA Modules:
  0.0 751.6 jit_solution(14504390201831847154)
XLA Ops:
  10.1 2.4 all_gather.34
  12.5 2.3 all_gather.30
  14.8 2.3 all_gather.31
  17.1 2.3 all_gather.32
  19.5 37.9 %all-gather.7.cloned.1.call-done = bf16[2048,768]{1,0:T(8,128)(2,1)} async-done(((bf16[512,768]{1,0:T(8,128)(2,1)}), bf16[2048,768]{1,0:T(8,128)(2,1)}) %all-gather.7.cloned.1.call-update) | async-done | bytes 3145744 | tf_op jit(solution)/shard_map/all_gather | solution.py:16
  57.4 3.9 fusion.63
  66.1 52.2 %while.27 = (s32[]{:T(128)}, bf16[4,512,192]{1,2,0:T(8,128)(2,1)}, f32[4,512,3]{1,2,0:T(4,128)S(1)}, s32[4]{0:T(128)S(1)}, s32[2048]{0:T(1024)S(1)}, /*index=5*/...) while((s32[]{:T(128)}, bf16[4,512,192]{1,2,0:T(8,128)(2,1)}, ...), condition=%wide.region_7.8_spmd, body=%wide.region_0.7_spmd.sunk | while | flops 843649024 | bytes 42000656 | solution.py:96
  67.4 1.9 fusion.158
  71.2 1.8 fusion.155
  74.8 1.8 fusion.161
  80.5 1.9 fusion.158
  84.3 1.8 fusion.155
  93.5 1.9 fusion.158
  97.3 1.8 fusion.155
  106.6 1.9 fusion.158
  110.4 1.8 fusion.155
  120.8 2.7 convolution_convert_fusion.3
  124.6 43.0 %reduce-scatter.21.cloned.1.call-done = bf16[512,768]{1,0:T(8,128)(2,1)} async-done(((bf16[2048,768]{1,0:T(8,128)(2,1)}), bf16[512,768]{1,0:T(8,128)(2,1)}) %reduce-scatter.21.cloned.1.call-update) | async-done | bytes 786448 | tf_op jit(solution)/shard_map/reduce_scatter | solution.py:20
  172.9 43.2 %all-gather.9.cloned.1.call-done = bf16[2048,768]{1,0:T(8,128)(2,1)} async-done(((bf16[512,768]{1,0:T(8,128)(2,1)}), bf16[2048,768]{1,0:T(8,128)(2,1)}) %all-gather.9.cloned.1.call-update) | async-done | bytes 3145744 | tf_op jit(solution)/shard_map/all_gather | solution.py:16
  216.1 7.0 multiply_convert_fusion.3
  223.0 3.6 all-gather.13.cloned.1.call-done
  226.6 6.5 convolution_convert_fusion.1
  234.4 43.8 %reduce-scatter.23.cloned.1.call-done = bf16[512,768]{1,0:T(8,128)(2,1)} async-done(((bf16[2048,768]{1,0:T(8,128)(2,1)}), bf16[512,768]{1,0:T(8,128)(2,1)}) %reduce-scatter.23.cloned.1.call-update) | async-done | bytes 786448 | tf_op jit(solution)/shard_map/reduce_scatter | solution.py:20
  278.2 2.3 fusion.69
  281.4 2.9 fusion.71
  284.3 3.0 convert_reduce_fusion.2
  287.4 44.1 %all-gather.15.cloned.1.call-done = bf16[2048,768]{1,0:T(8,128)(2,1)} async-done(((bf16[512,768]{1,0:T(8,128)(2,1)}), bf16[2048,768]{1,0:T(8,128)(2,1)}) %all-gather.15.cloned.1.call-update) | async-done | bytes 3145744 | tf_op jit(solution)/shard_map/all_gather | solution.py:16
  331.5 8.1 %convert_reduce_fusion = (f32[768]{0:T(1024)}, bf16[2048,768]{1,0:T(8,128)(2,1)S(1)}) fusion(f32[2048,768]{1,0:T(8,128)} %get-tuple-element.364, f32[768]{0:T(1024)S(1)} %convert_element_type.207, bf16[2048,768]{1,0:T(8,128)(2,1)} %all-gather.15.cloned.1.call-done, bf16[768,768]{1,0:T(8,128)(2,1)} %all-gather.13.cloned.1.call-done), kind=kOutput, calls=%fused_computation.103 | convolution fusion | flops 2436365568 | bytes 13768704 | tf_op jit(solution)/shard_map/lm,fm->lf/dot_general | solution.py:274
  341.2 4.0 convolution_convert_fusion
  345.3 43.9 %reduce-scatter.25.cloned.1.call-done = bf16[512,768]{1,0:T(8,128)(2,1)} async-done(((bf16[2048,768]{1,0:T(8,128)(2,1)}), bf16[512,768]{1,0:T(8,128)(2,1)}) %reduce-scatter.25.cloned.1.call-update) | async-done | bytes 786448 | tf_op jit(solution)/shard_map/reduce_scatter | solution.py:20
  389.2 3.5 multiply_reduce_fusion.4
  392.8 2.8 convert_reduce_fusion.3
  395.6 5.5 convolution_convert_fusion.5
  402.7 37.0 %all-gather.17.cloned.1.call-done = bf16[2048,768]{1,0:T(8,128)(2,1)} async-done(((bf16[512,768]{1,0:T(8,128)(2,1)}), bf16[2048,768]{1,0:T(8,128)(2,1)}) %all-gather.17.cloned.1.call-update) | async-done | bytes 3145744 | tf_op jit(solution)/shard_map/all_gather | solution.py:16
  439.7 4.0 convolution_convert_fusion.4
  444.6 106.6 %while.28 = (s32[]{:T(128)}, f32[2048,192]{0,1:T(8,128)}, f32[2048,192]{0,1:T(8,128)}, bf16[4,512,192]{1,2,0:T(8,128)(2,1)}, s32[4]{0:T(128)S(1)}, /*index=5*/s3...) while((s32[]{:T(128)}, f32[2048,192]{0,1:T(8,128)}, ...), condition=%wide.region_27.28_spmd.clone, body=%wide.region_23.27_spmd.clone.sunk | while | flops 2058486784 | bytes 141845040 | solution.py:165
  451.2 2.4 multiply_reduce_fusion.14
  456.7 2.5 multiply_reduce_fusion.15
  462.5 2.4 multiply_reduce_fusion.16
  477.8 2.4 multiply_reduce_fusion.14
  483.2 2.5 multiply_reduce_fusion.15
  489.1 2.4 multiply_reduce_fusion.16
  504.3 2.4 multiply_reduce_fusion.14
  509.8 2.5 multiply_reduce_fusion.15
  515.6 2.4 multiply_reduce_fusion.16
  530.9 2.4 multiply_reduce_fusion.14
  536.4 2.5 multiply_reduce_fusion.15
  542.2 2.4 multiply_reduce_fusion.16
  551.3 2.1 copy.80
  553.4 2.7 convolution_convert_fusion.8
  557.0 2.5 convert.16
  560.6 4.4 fusion.67
  568.0 6.5 convolution_convert_fusion.6
  574.7 2.2 copy.74
  581.0 9.4 %reduce-scatter.33.cloned.1.call-done = bf16[384,192]{1,0:T(8,128)(2,1)} async-done(((bf16[768,192]{1,0:T(8,128)(2,1)}), bf16[384,192]{1,0:T(8,128)(2,1)}) %reduce-scatter.33.cloned.1.call-update) | async-done | bytes 147472
  592.2 9.5 %reduce-scatter.31.cloned.1.call-done = bf16[384,192]{1,0:T(8,128)(2,1)} async-done(((bf16[768,192]{1,0:T(8,128)(2,1)}), bf16[384,192]{1,0:T(8,128)(2,1)}) %reduce-scatter.31.cloned.1.call-update) | async-done | bytes 147472
  603.3 10.9 %reduce-scatter.29.cloned.1.call-done = bf16[384,768]{1,0:T(8,128)(2,1)} async-done(((bf16[768,768]{1,0:T(8,128)(2,1)}), bf16[384,768]{1,0:T(8,128)(2,1)}) %reduce-scatter.29.cloned.1.call-update) | async-done | bytes 589840 | tf_op jit(solution)/shard_map/reduce_scatter | solution.py:328
  614.3 5.2 convolution_convert_fusion.2
  620.3 43.8 %all-reduce = (f32[]{:T(128)}, f32[]{:T(128)}, f32[768]{0:T(1024)}, f32[768]{0:T(1024)}, f32[768]{0:T(1024)}, /*index=5*/f32[768]{0:T(1024)}, f32[768]{0:T(1024)}, f32[768]{0:T(1024)}) all-reduce(f32[]{:T(128)} %get-tuple-element.262, f32[]{:T(128)} %get-tuple-element.334, ...), channel_id=1, replica_groups=mesh['gx'=4,'gy'=2,'gz'=4] {'gx','gy','gz'}, use_global_device_ids=true, to_apply=%region_15.16 | all-reduce | flops 4610 | bytes 36880 | tf_op jit(solution)/shard_map/psum | solution.py:360
  665.7 16.3 %all-reduce.1 = (f32[192]{0:T(256)}, f32[192]{0:T(256)}, f32[768]{0:T(1024)}) all-reduce(f32[192]{0:T(256)S(1)} %get-tuple-element.362, f32[192]{0:T(256)S(1)} %get-tuple-element.361, f32[768]{0:T(1024)S(1)} %copy-done.33), channel_id=1, replica_groups=mesh['gx'=4,'gy'=2,'gz'=4] {'gx','gy'}, use_global_device_ids=true, to_apply=%region_32.33 | all-reduce | flops 1152 | bytes 9216 | tf_op jit(solution)/shard_map/psum | solution.py:348
  682.0 12.6 %all-reduce.5.cloned.1.call-done = (bf16[384,192]{0,1:T(8,128)(2,1)}, bf16[384,192]{0,1:T(8,128)(2,1)}, bf16[384,192]{0,1:T(8,128)(2,1)}, bf16[192,384]{1,0:T(8,...) async-done(((bf16[384,192]{0,1:T(8,128)(2,1)}, bf16[384,192]{0,1:T(8,128)(2,1)}, bf16[384,192]{0,1:T(8,128)(2,1)}, bf16[192,384]{1,0:T(8,128)(2,1)}, ...) | async-done | bytes 1769488 | tf_op jit(solution)/shard_map/psum | solution.py:341
  701.4 2.2 convert_element_type.236
  704.6 35.9 %reduce-scatter.27.cloned.1.call-done = bf16[512,768]{1,0:T(8,128)(2,1)} async-done(((bf16[2048,768]{1,0:T(8,128)(2,1)}), bf16[512,768]{1,0:T(8,128)(2,1)}) %reduce-scatter.27.cloned.1.call-update) | async-done | bytes 786448 | tf_op jit(solution)/shard_map/reduce_scatter | solution.py:20
  740.5 2.2 add_convert_fusion.1
  (361 shorter events, 151.0 us)
Async XLA Ops:
  8.0 49.4 %all-gather.7.cloned.1.call-start = ((), (), s32[]{:S(2)}) async-start(), calls=%async_computation.10 | async-start | bytes 3932160 | tf_op jit(solution)/shard_map/all_gather | solution.py:16
  8.8 158.9 %reduce-scatter.21.cloned.1.call-start = ((), (), s32[]{:S(2)}) async-start(), calls=%async_computation.11 | async-start | bytes 3932160 | tf_op jit(solution)/shard_map/reduce_scatter | solution.py:20
  12.5 107.3 %copy-start.22 = (bf16[192,768]{1,0:T(8,128)(2,1)}, bf16[192,768]{1,0:T(8,128)(2,1)S(1)}, u32[]{:S(2)}) copy-start(bf16[192,768]{1,0:T(8,128)(2,1)S(1)} %all_gather.34) | copy-start | bytes 884740
  19.5 37.9 %copy-start.25 = (bf16[768,576]{0,1:T(8,128)(2,1)}, bf16[768,576]{0,1:T(8,128)(2,1)S(1)}, u32[]{:S(2)}) copy-start(bf16[768,576]{0,1:T(8,128)(2,1)S(1)} %constant_dynamic-update-slice_fusion) | copy-start | bytes 2654212
  63.1 2.9 copy-start.23
  63.1 2.9 copy-start.26
  118.2 1.6 copy-start.12
  123.5 1.1 copy-start.35
  123.5 1.1 copy-start.36
  123.5 44.2 %copy-start = (bf16[512,768]{1,0:T(8,128)(2,1)S(1)}, bf16[512,768]{1,0:T(8,128)(2,1)}, u32[]{:S(2)}) copy-start(bf16[512,768]{1,0:T(8,128)(2,1)} %param.24) | copy-start | bytes 2359300
  123.5 49.3 %all-gather.11.cloned.1.call-start = ((), (), s32[]{:S(2)}) async-start(), calls=%async_computation.13 | async-start | bytes 1769472 | tf_op jit(solution)/shard_map/all_gather | solution.py:206
  124.1 91.9 %all-gather.9.cloned.1.call-start = ((), (), s32[]{:S(2)}) async-start(), calls=%async_computation.12 | async-start | bytes 3932160 | tf_op jit(solution)/shard_map/all_gather | solution.py:16
  167.7 3.1 copy-start.6
  169.2 3.6 copy-start.37
  172.2 54.4 %all-gather.13.cloned.1.call-start = ((), (), s32[]{:S(2)}) async-start(), calls=%async_computation.14 | async-start | bytes 1769472 | tf_op jit(solution)/shard_map/all_gather | solution.py:210
  172.8 105.5 %reduce-scatter.23.cloned.1.call-start = ((), (), s32[]{:S(2)}) async-start(), calls=%async_computation.15 | async-start | bytes 3932160 | tf_op jit(solution)/shard_map/reduce_scatter | solution.py:20
  233.1 98.4 %all-gather.15.cloned.1.call-start = ((), (), s32[]{:S(2)}) async-start(), calls=%async_computation.16 | async-start | bytes 3932160 | tf_op jit(solution)/shard_map/all_gather | solution.py:16
  278.2 2.3 copy-start.7
  278.2 2.3 copy-start.14
  278.2 3.2 copy-start.17
  278.2 3.2 copy-start.18
  287.4 101.8 %reduce-scatter.25.cloned.1.call-start = ((), (), s32[]{:S(2)}) async-start(), calls=%async_computation.17 | async-start | bytes 3932160 | tf_op jit(solution)/shard_map/reduce_scatter | solution.py:20
  331.5 9.7 %copy-start.41 = (bf16[768,768]{1,0:T(8,128)(2,1)S(1)}, bf16[768,768]{1,0:T(8,128)(2,1)}, u32[]{:S(2)}) copy-start(bf16[768,768]{1,0:T(8,128)(2,1)} %all-gather.11.cloned.1.call-done) | copy-start | bytes 3538948
  339.6 1.7 copy-start.42
  345.3 94.4 %all-gather.17.cloned.1.call-start = ((), (), s32[]{:S(2)}) async-start(), calls=%async_computation.18 | async-start | bytes 3932160 | tf_op jit(solution)/shard_map/all_gather | solution.py:16
  389.2 3.6 copy-start.8
  389.2 3.6 copy-start.9
  389.2 3.6 copy-start.21
  395.6 179.1 %reduce-scatter.39.cloned.1.call-start = ((), (), s32[]{:S(2)}) async-start(), calls=%async_computation.25 | async-start | bytes 1769472
  402.6 174.3 %reduce-scatter.37.cloned.1.call-start = ((), (), s32[]{:S(2)}) async-start(), calls=%async_computation.24 | async-start | bytes 589824
  444.6 108.7 %copy-start.11 = (bf16[4,24,8,512]{3,2,0,1:T(8,128)(2,1)S(1)}, bf16[4,24,8,512]{3,2,0,1:T(8,128)(2,1)}, u32[]{:S(2)}) copy-start(bf16[4,24,8,512]{3,2,0,1:T(8,128)(2,1)} %copy-done.10) | copy-start | bytes 2359300
  449.5 1.7 copy-start.13
  466.7 1.4 copy-start.1
  466.7 1.9 copy-start.4
  469.6 1.3 copy-start.2
  469.7 1.7 copy-start.5
  476.1 1.7 copy-start.13
  493.2 1.4 copy-start.1
  493.2 1.9 copy-start.4
  496.2 1.3 copy-start.2
  496.2 1.7 copy-start.5
  502.6 1.7 copy-start.13
  519.8 1.4 copy-start.1
  519.8 1.9 copy-start.4
  522.8 1.3 copy-start.2
  522.8 1.7 copy-start.5
  529.2 1.7 copy-start.13
  546.4 1.4 copy-start.1
  546.4 1.9 copy-start.4
  549.3 1.3 copy-start.2
  549.3 1.7 copy-start.5
  556.0 3.4 copy-start.3
  557.0 3.5 copy-start.16
  560.5 18.8 %reduce-scatter.35.cloned.1.call-start = ((), (), s32[]{:S(2)}) async-start(), calls=%async_computation.23 | async-start | bytes 589824
  565.9 24.5 %reduce-scatter.33.cloned.1.call-start = ((), (), s32[]{:S(2)}) async-start(), calls=%async_computation.22 | async-start | bytes 589824
  566.9 34.7 %reduce-scatter.31.cloned.1.call-start = ((), (), s32[]{:S(2)}) async-start(), calls=%async_computation.21 | async-start | bytes 589824
  568.0 46.2 %reduce-scatter.29.cloned.1.call-start = ((), (), s32[]{:S(2)}) async-start(), calls=%async_computation.20 | async-start | bytes 1769472 | tf_op jit(solution)/shard_map/reduce_scatter | solution.py:328
  574.6 39.7 %copy-start.19 = (bf16[2048,192]{0,1:T(8,128)(2,1)S(1)}, bf16[2048,192]{0,1:T(8,128)(2,1)}, u32[]{:S(2)}) copy-start(bf16[2048,192]{0,1:T(8,128)(2,1)} %convert.16) | copy-start | bytes 2359300
  574.6 39.7 %copy-start.20 = (bf16[2048,192]{0,1:T(8,128)(2,1)S(1)}, bf16[2048,192]{0,1:T(8,128)(2,1)}, u32[]{:S(2)}) copy-start(bf16[2048,192]{0,1:T(8,128)(2,1)} %convert.17) | copy-start | bytes 2359300
  574.6 120.0 %all-reduce.5.cloned.1.call-start = ((), (), s32[]{:S(2)}) async-start(), calls=%async_computation.26 | async-start | bytes 3538944 | tf_op jit(solution)/shard_map/psum | solution.py:341
  614.2 126.3 %reduce-scatter.27.cloned.1.call-start = ((), (), s32[]{:S(2)}) async-start(), calls=%async_computation.19 | async-start | bytes 3932160 | tf_op jit(solution)/shard_map/reduce_scatter | solution.py:20
  619.5 46.2 %copy-start.33 = (f32[768]{0:T(1024)S(1)}, f32[768]{0:T(1024)}, u32[]{:S(2)}) copy-start(f32[768]{0:T(1024)} %get-tuple-element.365) | copy-start | bytes 9220
  694.6 8.9 %copy-start.24 = (bf16[768,384]{1,0:T(8,128)(2,1)S(1)}, bf16[768,384]{1,0:T(8,128)(2,1)}, u32[]{:S(2)}) copy-start(bf16[768,384]{1,0:T(8,128)(2,1)} %get-tuple-element.327) | copy-start | bytes 1769476
  696.3 44.2 %copy-start.15 = (f32[512,768]{1,0:T(8,128)S(1)}, f32[512,768]{1,0:T(8,128)}, u32[]{:S(2)}) copy-start(f32[512,768]{1,0:T(8,128)} %get-tuple-element.333) | copy-start | bytes 4718596
  (11 other events, 8.4 us)
Sparse Core Ops, SparseCore 0:
  10.7 46.6 all-gather.6
  123.7 43.9 reduce-scatter.20
  287.5 43.9 all-gather.14
  395.7 43.9 all-gather.16
  614.3 80.2 all-reduce.4
  697.7 42.7 reduce-scatter.26
Sparse Core Ops, SparseCore 1:
  125.5 9.1 all-gather.10
  172.3 43.7 all-gather.8
  217.5 9.1 all-gather.12
  233.2 45.0 reduce-scatter.22
  345.4 43.8 reduce-scatter.24
  402.7 8.6 reduce-scatter.38
  560.6 7.7 reduce-scatter.36
  570.4 8.8 reduce-scatter.34
  581.5 8.8 reduce-scatter.32
  592.7 8.8 reduce-scatter.30
  604.4 9.7 reduce-scatter.28
where the time goes:
time: 756 us; the launch traced here: 752 us
  waiting for transfers between devices  377 us (50%)
  matrix products  177 us (23%)
  blocking collectives  69.3 us (9%)
  other arithmetic  62.3 us (8%)
  local copies, waits for them, and re-layouts  39.4 us (5%)
  between operations  19 us (3%)
    reduce_scatter x4, waiting for transfers between devices, sum_rows(): lax.psum_scatter(term_fn(jnp.int32(0), lax.axis_size('gz') * row_count).a...  167 us
    all_gather x4, waiting for transfers between devices, gather_rows(): return lax.all_gather(tensor, 'gz', axis=0, tiled=True)  162 us
    dot_general x24, matrix products, one_block(): jnp.einsum('qd,kd->qk', query_block[:, columns], key_rows[:, columns], pr...  50.6 us
    psum x1, blocking collectives, shards(): lax.psum((d_norm1_gain, d_norm1_bias, d_norm2_gain, d_norm2_bias, d_b_out...  43.8 us
    unnamed x22, waiting for transfers between devices  21.5 us
    dot_general x12, matrix products, one_block(): jnp.einsum('qd,kd->qk', grad_block[:, columns], value_rows[:, columns], p...  19.6 us
    unnamed x88, local copies, waits for them, and re-layouts  18.3 us
    psum x1, blocking collectives, shards(): lax.psum((d_bias_qkv[:col_width], d_bias_qkv[2 * col_width:], d_bias_up),...  16.3 us
  transfers between devices with their start and end apart: 17, of which 14 were waited for; matrix products, arithmetic and copies ran while one was open for 23% of the time, Pallas kernels for 0%

commit v1 on v0

v1 whole, which is shorter than its diff:
```python
import math

import jax
import jax.numpy as jnp
from jax import lax
from jax.experimental import pallas as pl
from jax.experimental.pallas import tpu as pltpu
from jax.sharding import PartitionSpec as P

EPSILON = 1e-05
MASKED = -1e30
PAD_ROWS = 16
BLK = 256
F32 = jnp.float32
BF16 = jnp.bfloat16
NT = (((1,), (1,)), ((), ()))
NN = (((1,), (0,)), ((), ()))

def norm_forward(resid, gain, shift):
    average = jnp.mean(resid, -1, keepdims=True)
    centered = resid - average
    inv_std = lax.rsqrt(jnp.mean(centered * centered, -1, keepdims=True) + EPSILON)
    normed = centered * inv_std
    return (normed * gain + shift, normed, inv_std)


def norm_backward(upstream, normed, inv_std, gain):
    d_gain = jnp.sum(upstream * normed, 0)
    d_shift = jnp.sum(upstream, 0)
    scaled = upstream * gain
    d_resid = inv_std * (
        scaled
        - jnp.mean(scaled, -1, keepdims=True)
        - normed * jnp.mean(scaled * normed, -1, keepdims=True)
    )
    return (d_resid, d_gain, d_shift)


def gelu_parts(preact):
    normal_cdf = 0.5 * (1.0 + lax.erf(preact * (1.0 / math.sqrt(2.0))))
    slope = normal_cdf + preact * jnp.exp(-0.5 * preact * preact) * (1.0 / math.sqrt(2.0 * math.pi))
    return (preact * normal_cdf, slope)


def dot(a,b,dims=NN):
    return lax.dot_general(a,b,dims,preferred_element_type=F32)

def split3(v):
    hi=v.astype(BF16); r=v-hi.astype(F32); mid=r.astype(BF16); lo=(r-mid.astype(F32)).astype(BF16)
    return hi,mid,lo

def fwd_kernel(bounds, t0,t1,t2,t3, wa, wb, encq, enck, vrow, a0,a1,a2,a3, qp,kp,vp,op, wp, bias, s_scr, m_scr, acc_scr):
    heads=3
    half=wa.shape[0]-16
    b0=bounds[2,0]
    lane=lax.broadcasted_iota(jnp.int32,(BLK,128),1)
    wp[...]=jnp.zeros_like(wp)
    for i in range(9):
        wp[:half,i*128:i*128+64]=wa[:half,i*64:(i+1)*64]
        wp[half:,i*128:i*128+64]=wb[:half,i*64:(i+1)*64]
    bias[...]=jnp.zeros_like(bias)
    for i in range(9):
        bias[:,i*128:i*128+64]=wa[half:half+1,i*64:(i+1)*64].astype(F32)
    encv=jnp.where((lane>=64)&(lane<67),1.0,0.0).astype(BF16)
    for kk,t in enumerate((t0,t1,t2,t3)):
        nb=t.shape[0]//BLK
        for r in range(nb):
            rows=slice(kk*t.shape[0]+r*BLK, kk*t.shape[0]+(r+1)*BLK)
            x=t[r*BLK:(r+1)*BLK,:]
            y=dot(x,wp[...])+bias[...]
            for h in range(heads):
                qp[h,rows,:]=y[:,h*128:(h+1)*128].astype(BF16)*jnp.asarray(0.125,BF16)+encq[rows,:]
                kp[h,rows,:]=y[:,(3+h)*128:(4+h)*128].astype(BF16)+enck[rows,:]
                vp[h,rows,:]=y[:,(6+h)*128:(7+h)*128].astype(BF16)+encv
    nblk=qp.shape[1]//BLK
    eye=lax.broadcasted_iota(jnp.int32,(BLK,BLK),0)==lax.broadcasted_iota(jnp.int32,(BLK,BLK),1)
    nolane80=jnp.where(lane==80,0.0,1.0).astype(BF16)
    def relrow(j):
        return pl.multiple_of((j ^ (2*b0))*BLK, BLK)
    def qblock(i,_):
        rows=pl.ds(relrow(i),BLK)
        lo=bounds[0,i]; hi=bounds[1,i]
        below=jnp.maximum(jnp.minimum(hi,i)-lo,0); above=jnp.maximum(hi-(i+1),0)
        cnt=below+above
        ok=(vrow[pl.ds(i ^ (2*b0),1),:]>0)|eye
        for h in range(heads):
            s=dot(qp[h,rows,:]*nolane80,kp[h,rows,:],NT)
            s=jnp.where(ok,s,MASKED)
            s_scr[h,0]=s
            m_scr[h]=jnp.maximum(s[:,:128],s[:,128:])
        def jof(t):
            return jnp.where(t<below, lo+t, i+1+t-below)
        def l1(t,_):
            kr=pl.ds(relrow(jof(t)),BLK)
            for h in range(heads):
                s=dot(qp[h,rows,:],kp[h,kr,:],NT)
                s_scr[h,t+1]=s
                m_scr[h]=jnp.maximum(m_scr[h],jnp.maximum(s[:,:128],s[:,128:]))
            return 0
        lax.fori_loop(0,cnt,l1,0)
        for h in range(heads):
            m=jnp.max(m_scr[h],axis=1,keepdims=True)
            m_scr[h]=jnp.broadcast_to(m,(BLK,128))
        for h in range(heads):
            m=m_scr[h]
            p=jnp.exp(s_scr[h,0]-jnp.concatenate([m,m],1)).astype(BF16)
            acc_scr[h]=dot(p,vp[h,rows,:])
        def l2(t,_):
            kr=pl.ds(relrow(jof(t)),BLK)
            for h in range(heads):
                m=m_scr[h]
                p=jnp.exp(s_scr[h,t+1]-jnp.concatenate([m,m],1)).astype(BF16)
                acc_scr[h]+=dot(p,vp[h,kr,:])
            return 0
        lax.fori_loop(0,cnt,l2,0)
        os=[]
        for h in range(heads):
            acc=acc_scr[h]
            l=acc[:,64:65]
            o=acc*(1.0/l)
            op[h,rows,:]=o
            os.append(o.astype(BF16).astype(F32))
            L=m_scr[h][:,0:1]+jnp.log(l)
            hi_,mid_,lo_=split3(L)
            zero=jnp.zeros((BLK,128),F32)
            add=jnp.where(lane==81,hi_.astype(F32),jnp.where(lane==82,mid_.astype(F32),jnp.where(lane==83,lo_.astype(F32),zero)))
            qp[h,rows,:]=qp[h,rows,:]+add.astype(BF16)
        o01=jnp.where(lane<64,os[0],pltpu.roll(os[1],64,1)).astype(BF16)
        o2=os[2][:,:64].astype(BF16)
        ri=i ^ (2*b0)
        for kk,a in enumerate((a0,a1,a2,a3)):
            @pl.when(ri//2==kk)
            def _():
                rr=pl.ds(pl.multiple_of((ri%2)*BLK,BLK),BLK)
                a[rr,0:128]=o01
                a[rr,128:192]=o2
        return 0
    lax.fori_loop(0,nblk,qblock,0)

def bwd_kernel(bounds, d0,d1,d2,d3, qp,kp,vp,op, vrow, dq_o,dk_o,dv_o, dop, dq_s, dk_s, dv_s):
    heads=3
    b0=bounds[2,0]
    lane=lax.broadcasted_iota(jnp.int32,(BLK,128),1)
    zero64=jnp.zeros((BLK,64),BF16)
    for kk,d in enumerate((d0,d1,d2,d3)):
        for r in range(d.shape[0]//BLK):
            rows=slice(kk*d.shape[0]+r*BLK, kk*d.shape[0]+(r+1)*BLK)
            x01=d[r*BLK:(r+1)*BLK,0:128].astype(F32)
            x2=jnp.concatenate([d[r*BLK:(r+1)*BLK,128:192],zero64],1).astype(F32)
            xs=[jnp.where(lane<64,x01,0.0),jnp.where(lane<64,pltpu.roll(x01,64,1),0.0),x2]
            for h in range(heads):
                delta=jnp.sum(xs[h]*op[h,rows,:],axis=1,keepdims=True)
                hi_,mid_,lo_=split3(-delta)
                v=jnp.where(lane==64,hi_.astype(F32),jnp.where(lane==65,mid_.astype(F32),jnp.where(lane==66,lo_.astype(F32),xs[h])))
                dop[h,rows,:]=v.astype(BF16)
    dk_s[...]=jnp.zeros_like(dk_s)
    dv_s[...]=jnp.zeros_like(dv_s)
    nblk=qp.shape[1]//BLK
    eye=lax.broadcasted_iota(jnp.int32,(BLK,BLK),0)==lax.broadcasted_iota(jnp.int32,(BLK,BLK),1)
    nolane80=jnp.where(lane==80,0.0,1.0).astype(BF16)
    def relrow(j):
        return pl.multiple_of((j ^ (2*b0))*BLK, BLK)
    TN=(((0,),(0,)),((),()))
    def pair(h,rows,kr,diag_ok=None):
        q=qp[h,rows,:]; d=dop[h,rows,:]; k=kp[h,kr,:]; v=vp[h,kr,:]
        if diag_ok is None:
            s=dot(q,k,NT)
        else:
            s=dot(q*nolane80,k,NT)
            s=jnp.where(diag_ok,s,MASKED)
        p=jnp.exp(s)
        dp=dot(d,v,NT)
        ds=(p*dp).astype(BF16); pb=p.astype(BF16)
        dv_s[h,kr,:]+=dot(pb,d,TN)
        dk_s[h,kr,:]+=dot(ds,q,TN)
        return dot(ds,k)
    def qblock(i,_):
        rows=pl.ds(relrow(i),BLK)
        lo=bounds[0,i]; hi=bounds[1,i]
        below=jnp.maximum(jnp.minimum(hi,i)-lo,0); above=jnp.maximum(hi-(i+1),0)
        cnt=below+above
        ok=(vrow[pl.ds(i ^ (2*b0),1),:]>0)|eye
        for h in range(heads):
            dq_s[h]=pair(h,rows,rows,ok)
        def l1(t,_):
            j=jnp.where(t<below, lo+t, i+1+t-below)
            kr=pl.ds(relrow(j),BLK)
            for h in range(heads):
                dq_s[h]+=pair(h,rows,kr)
            return 0
        lax.fori_loop(0,cnt,l1,0)
        q=[dq_s[h]*0.125 for h in range(3)]
        dq_o[rows,0:128]=jnp.where(lane<64,q[0],pltpu.roll(q[1],64,1)).astype(BF16)
        dq_o[rows,128:192]=q[2][:,:64].astype(BF16)
        return 0
    lax.fori_loop(0,nblk,qblock,0)
    for src,dst in ((dk_s,dk_o),(dv_s,dv_o)):
        for r in range(nblk):
            rows=slice(r*BLK,(r+1)*BLK)
            dst[rows,0:128]=jnp.where(lane<64,src[0,rows,:],pltpu.roll(src[1,rows,:],64,1)).astype(BF16)
            dst[rows,128:192]=src[2,rows,:][:,:64].astype(BF16)

VM=pl.BlockSpec(memory_space=pltpu.VMEM)
SM=pl.BlockSpec(memory_space=pltpu.SMEM)
def attention_forward(bounds,ts,wa,wb,encq,enck,vrow):
    n=ts[0].shape[0]*4; d=ts[0].shape[1]
    S=jax.ShapeDtypeStruct
    return pl.pallas_call(fwd_kernel,
        out_shape=[S((n//4,192),BF16)]*4+[S((3,n,128),BF16)]*3+[S((3,n,128),F32)],
        in_specs=[SM]+[VM]*9, out_specs=[VM]*8,
        scratch_shapes=[pltpu.VMEM((d,1152),BF16),pltpu.VMEM((1,1152),F32),pltpu.VMEM((3,n//BLK,BLK,BLK),F32),pltpu.VMEM((3,BLK,128),F32),pltpu.VMEM((3,BLK,128),F32)],
        compiler_params=pltpu.CompilerParams(vmem_limit_bytes=52<<20),
        name="attn_fwd")(bounds,*ts,wa,wb,encq,enck,vrow)
def attention_backward(bounds,ds,qp,kp,vp,op,vrow):
    n=qp.shape[1]
    S=jax.ShapeDtypeStruct
    return pl.pallas_call(bwd_kernel,
        out_shape=[S((n,192),BF16)]*3,
        in_specs=[SM]+[VM]*9, out_specs=[VM]*3,
        scratch_shapes=[pltpu.VMEM((3,n,128),BF16),pltpu.VMEM((3,BLK,128),F32),pltpu.VMEM((3,n,128),F32),pltpu.VMEM((3,n,128),F32)],
        compiler_params=pltpu.CompilerParams(vmem_limit_bytes=52<<20),
        name="attn_bwd")(bounds,*ds,qp,kp,vp,op,vrow)

def mask_tables(code, b0):
    n=code.shape[0]; nb=n//BLK
    seg=code//2; val=code%2
    first=seg[::BLK]; last=seg[BLK-1::BLK]
    lo=jnp.sum(last[None,:]<first[:,None],1)
    nvalid=jnp.sum(val)
    hi=jnp.minimum(jnp.sum(first[None,:]<=last[:,None],1),(nvalid+BLK-1)//BLK)
    b0v=jnp.zeros((nb,),jnp.int32)+b0
    bounds=jnp.stack([lo.astype(jnp.int32),hi.astype(jnp.int32),b0v])
    idx=jnp.arange(4,dtype=jnp.int32)^b0
    crel=jnp.take(code.reshape(4,n//4),idx,axis=0).reshape(n)
    segr=(crel//2)[:,None]; valr=(crel%2)[:,None]
    lane=jnp.arange(128,dtype=jnp.int32)[None,:]
    inoh=(lane>=64)&(lane<80)
    same=(lane-64)==segr
    encq=jnp.where((inoh&same)|(lane==80),1.0,0.0).astype(BF16)
    enck=jnp.where((inoh&~same)|((lane==80)&(valr==0)),MASKED,jnp.where((lane>=81)&(lane<84),-1.0,0.0)).astype(BF16)
    vrow=(crel%2).reshape(nb,BLK)
    return bounds,encq,enck,vrow


def gate_halves(flip, value):
    half = value.shape[-1] // 2
    swapped = jnp.concatenate([value[..., half:], value[..., :half]], -1)
    return jnp.where(flip, swapped, value)


def plane_perm(to):
    return [
        (
            core * 4 + row * 2 + col,
            (lambda t: t[0] * 4 + t[1] * 2 + t[2])(to(core, row, col)),
        )
        for core in range(2)
        for row in range(2)
        for col in range(2)
    ]


CORE_CHIP = ("gy", "gz")
TO_OWNER = [
    plane_perm(lambda core, row, col, a=k // 2, b=k % 2: (row, core ^ a, col ^ b))
    for k in range(4)
]
TO_HEADS = [
    plane_perm(lambda core, row, col, a=k // 2, b=k % 2: (row ^ a, core, col ^ b))
    for k in range(4)
]
CHIP = [[(c, c ^ k) for c in range(4)] for k in range(4)]
CORE = [(0, 1), (1, 0)]


def to_owner(value, k):
    return lax.ppermute(value, CORE_CHIP, TO_OWNER[k])


def to_heads(value, k):
    return lax.ppermute(value, CORE_CHIP, TO_HEADS[k])


def to_chip(value, k):
    return lax.ppermute(value, "gz", CHIP[k])


def to_core(value):
    return lax.ppermute(value, "gy", CORE)


def gather_chips(own):
    half = own.shape[0] // 2
    along_x = to_chip(own, 1)
    along_y = to_chip(own, 2)
    first = to_chip(along_x[:half], 2)
    second = to_chip(along_y[half:], 1)
    return own, along_x, along_y, jnp.concatenate([first, second], 0)


def add_low(left, right):
    return (left.astype(F32) + right.astype(F32)).astype(BF16)


def scatter_chips(pieces):
    half = pieces[0].shape[0] // 2
    upper = [piece[:half] for piece in pieces]
    lower = [piece[half:] for piece in pieces]
    came_x = to_chip(jnp.stack([upper[1], upper[3]]), 1)
    came_y = to_chip(jnp.stack([lower[2], lower[3]]), 2)
    upper_y = to_chip(add_low(upper[2], came_x[1]), 2)
    lower_x = to_chip(add_low(lower[1], came_y[1]), 1)
    upper_sum = upper[0].astype(F32) + came_x[0].astype(F32) + upper_y.astype(F32)
    lower_sum = lower[0].astype(F32) + came_y[0].astype(F32) + lower_x.astype(F32)
    return jnp.concatenate([upper_sum, lower_sum], 0)


def sum_all(vectors):
    vectors = vectors + to_core(vectors)
    swap = jnp.array
    fixed, spread = vectors[:-4], vectors[-4:]
    for k in (1, 2):
        came = to_chip(jnp.concatenate([fixed, spread], 0), k)
        fixed = fixed + came[:-4]
        other = came[-4:]
        if k == 1:
            other = jnp.concatenate([other[1:2], other[0:1], other[3:4], other[2:3]], 0)
        else:
            other = jnp.concatenate([other[2:4], other[0:2]], 0)
        spread = spread + other
    total = jnp.concatenate([fixed, spread[:1]], 0)
    planes = lax.axis_size("gx")
    if planes & (planes - 1):
        return lax.psum(total, "gx")
    step = 1
    while step < planes:
        total = total + lax.ppermute(total, "gx", [(p, p ^ step) for p in range(planes)])
        step *= 2
    return total


def shards(
    tokens,
    segment_ids,
    valid_mask,
    cotangent,
    teacher,
    w_query,
    b_query,
    w_key,
    w_value,
    b_value,
    w_out,
    b_out,
    norm1_gain,
    norm1_bias,
    w_up,
    b_up,
    w_down,
    b_down,
    norm2_gain,
    norm2_bias,
):
    row_count, width = tokens.shape
    half = width // 2
    core = lax.axis_index("gy")
    chip = lax.axis_index("gz")
    flip = core == 1
    block_col = w_query.shape[1]

    valid_row = valid_mask[0]
    own_valid = lax.dynamic_slice_in_dim(valid_row, chip * row_count, row_count).astype(F32)[:, None]

    own_tokens = gate_halves(flip, tokens)
    shard0 = to_owner(own_tokens, 0)
    shard1 = to_owner(own_tokens, 1)
    code = to_owner(segment_ids * 2 + valid_mask, 0)
    qkv_own = jnp.concatenate([w_query, w_key, w_value], 1)
    qkv_bias = jnp.concatenate([b_query, jnp.zeros_like(b_query), b_value])[None, :]
    qkv_own = jnp.concatenate([qkv_own, jnp.broadcast_to(qkv_bias, (PAD_ROWS, 3 * block_col))], 0)
    qkv_other = to_core(qkv_own)
    qkv_a = to_owner(qkv_own, 0)
    qkv_b = to_owner(qkv_other, 0)
    shard2 = to_core(shard0)
    shard3 = to_core(shard1)
    token_shards = (shard0, shard1, shard2, shard3)

    out_own = jnp.concatenate([w_out] + [to_chip(w_out, k) for k in (1, 2, 3)], 0)
    out_full = jnp.concatenate([out_own, to_core(out_own)], 1)
    up_ext = jnp.concatenate([w_up, jnp.broadcast_to(b_up[None, :], (PAD_ROWS, w_up.shape[1]))], 0)
    up_own = jnp.concatenate(gather_chips(up_ext), 1)
    up_other = to_core(up_own[:half])
    up_full = jnp.concatenate([up_own[:half], up_other], 0)
    up_bias = up_own[half].astype(F32)
    down_own = jnp.concatenate(gather_chips(w_down), 0)
    down_full = jnp.concatenate([down_own, to_core(down_own)], 1)

    head_block = core * 2 + chip % 2
    bounds, enc_query, enc_key, valid_rows = mask_tables(code[0], head_block)
    results = attention_forward(
        bounds, token_shards, qkv_a, qkv_b, enc_query, enc_key, valid_rows
    )
    query_pad, key_pad, value_pad, normed_out = results[4:]
    attended = jnp.concatenate([to_owner(results[k], k) for k in range(4)], 1)

    gain1, shift1, gain2, shift2, bias_out, bias_down = (
        gate_halves(flip, v.astype(F32))
        for v in (norm1_gain, norm1_bias, norm2_gain, norm2_bias, b_out, b_down)
    )
    own_cotangent = gate_halves(flip, cotangent)
    own_teacher = gate_halves(flip, teacher)
    mixed = jnp.dot(attended, out_full, preferred_element_type=F32) + bias_out
    resid1 = own_tokens.astype(F32) + mixed
    hidden, normed1, inv_std1 = norm_forward(resid1, gain1, shift1)
    hidden_low = hidden.astype(BF16)
    preact = jnp.dot(hidden_low, up_full, preferred_element_type=F32) + up_bias
    activated, slope = gelu_parts(preact)
    activated = activated.astype(BF16)
    slope = slope.astype(BF16)
    branch = jnp.dot(activated, down_full, preferred_element_type=F32)
    resid2 = hidden + (branch + bias_down)
    output_full, normed2, inv_std2 = norm_forward(resid2, gain2, shift2)
    mismatch = output_full - own_teacher.astype(F32)
    error_part = jnp.sum(own_valid * mismatch * mismatch)
    count_part = jnp.sum(own_valid)
    d_output = own_cotangent.astype(F32) + own_valid * mismatch
    d_resid2, d_gain2, d_shift2 = norm_backward(d_output, normed2, inv_std2, gain2)
    d_branch = d_resid2.astype(BF16)
    d_b_down = jnp.sum(d_branch, 0, dtype=F32)
    d_act = jnp.einsum("lm,fm->lf", d_branch, down_full, preferred_element_type=F32)
    d_pre = (d_act * slope.astype(F32)).astype(BF16)
    d_b_up = jnp.sum(d_pre, 0, dtype=F32)
    d_hidden = d_resid2 + jnp.einsum("lf,mf->lm", d_pre, up_full, preferred_element_type=F32)
    d_resid1, d_gain1, d_shift1 = norm_backward(d_hidden, normed1, inv_std1, gain1)
    d_mixed = d_resid1.astype(BF16)
    d_b_out = jnp.sum(d_mixed, 0, dtype=F32)
    d_attended = jnp.einsum(
        "lm,cm->lc", d_mixed, out_full, preferred_element_type=F32
    ).astype(BF16)
    d_pieces = [
        to_heads(d_attended[:, k * block_col : (k + 1) * block_col], k) for k in range(4)
    ]

    d_down = jnp.einsum("lf,lm->fm", activated, d_branch, preferred_element_type=F32).astype(BF16)
    d_up = jnp.einsum("lm,lf->mf", hidden_low, d_pre, preferred_element_type=F32).astype(BF16)
    d_out = jnp.einsum("lc,lm->cm", attended, d_mixed, preferred_element_type=F32).astype(BF16)
    d_down = add_low(d_down[:, :half], to_core(d_down[:, half:]))
    d_up = add_low(d_up[:half], to_core(d_up[half:]))
    d_out = add_low(d_out[:, :half], to_core(d_out[:, half:]))
    hidden_col = w_up.shape[1]
    grad_down = scatter_chips([d_down[k * hidden_col : (k + 1) * hidden_col] for k in range(4)])
    grad_up = scatter_chips([d_up[:, k * hidden_col : (k + 1) * hidden_col] for k in range(4)])
    grad_out = d_out[:block_col].astype(F32)
    for k in (1, 2, 3):
        grad_out = grad_out + to_chip(d_out[k * block_col : (k + 1) * block_col], k).astype(F32)
    grad_down, grad_up, grad_out = (
        lax.psum(v.astype(BF16), "gx").astype(F32) for v in (grad_down, grad_up, grad_out)
    )

    vectors = [gate_halves(flip, v) for v in (d_gain1, d_shift1, d_gain2, d_shift2, d_b_out, d_b_down)]
    scalars = jnp.concatenate([error_part[None], count_part[None], jnp.zeros((width - 2,), F32)])
    table = jnp.concatenate(
        [jnp.stack(vectors + [scalars]), d_b_up.reshape(4, hidden_col)], 0
    )
    sums = sum_all(table)

    d_query, d_key, d_value = attention_backward(
        bounds, d_pieces, query_pad, key_pad, value_pad, normed_out, valid_rows
    )
    d_qkv = jnp.concatenate([d_query, d_key, d_value], 1)
    qkv_full = jnp.concatenate([qkv_a[:half], qkv_b[:half]], 0)
    term = jnp.einsum("lc,mc->lm", d_qkv, qkv_full, preferred_element_type=F32).astype(BF16)
    group = 2 * row_count
    term = add_low(term[:group], to_core(term[group:]))
    d_tokens = (
        d_resid1
        + to_owner(term[:row_count], 0).astype(F32)
        + to_owner(term[row_count:], 1).astype(F32)
    )
    d_w = jnp.einsum(
        "lm,lc->mc", jnp.concatenate(token_shards, 0), d_qkv, preferred_element_type=F32
    ).astype(BF16)
    d_bias = jnp.sum(d_qkv, 0, dtype=F32)[None, :]
    d_bias_high = d_bias.astype(BF16)
    d_bias_low = (d_bias - d_bias_high.astype(F32)).astype(BF16)
    bias_rows = jnp.concatenate(
        [d_bias_high, d_bias_low, jnp.zeros((PAD_ROWS - 2, 3 * block_col), BF16)], 0
    )
    d_w = to_owner(jnp.concatenate([d_w[:half], bias_rows, d_w[half:], bias_rows], 0), 0)
    split = half + PAD_ROWS
    d_w = add_low(d_w[:split], to_core(d_w[split:]))
    d_w = lax.psum(d_w, "gx").astype(F32)
    grad_qkv = d_w[:half]
    grad_bias = d_w[half] + d_w[half + 1]

    mean_loss = sums[6, 0] / (sums[6, 1] * width)
    return (
        gate_halves(flip, output_full.astype(BF16)),
        mean_loss,
        gate_halves(flip, d_tokens.astype(BF16)),
        grad_qkv[:, :block_col],
        grad_bias[:block_col],
        grad_qkv[:, block_col : 2 * block_col],
        grad_qkv[:, 2 * block_col :],
        grad_bias[2 * block_col :],
        grad_out,
        sums[4],
        sums[0],
        sums[1],
        grad_up,
        sums[7],
        grad_down,
        sums[5],
        sums[2],
        sums[3],
    )


def solution(mesh):
    placed = (
        P(("gx", "gy", "gz"), None),
        P(("gx", "gy"), None),
        P(("gx", "gy"), None),
        P(("gx", "gy", "gz"), None),
        P(("gx", "gy", "gz"), None),
        P("gy", "gz"),
        P("gz"),
        P("gy", "gz"),
        P("gy", "gz"),
        P("gz"),
        P("gz", "gy"),
        P(),
        P(),
        P(),
        P("gy", "gz"),
        P("gz"),
        P("gz", "gy"),
        P(),
        P(),
        P(),
    )
    return jax.shard_map(
        shards,
        mesh=mesh,
        in_specs=placed,
        out_specs=(
            P(("gx", "gy", "gz"), None),
            P(),
            P(("gx", "gy", "gz"), None),
            P("gy", "gz"),
            P("gz"),
            P("gy", "gz"),
            P("gy", "gz"),
            P("gz"),
            P("gz", "gy"),
            P(),
            P(),
            P(),
            P("gy", "gz"),
            P("gz"),
            P("gz", "gy"),
            P(),
            P(),
            P(),
        ),
        check_vma=False,
    )
```

time: 756 us -> 514 us (0.68)
  waiting for transfers between devices: 377 us -> 160 us
  matrix products: 177 us -> 45.6 us
  starting transfers between devices: 1.12 us -> 109 us
  blocking collectives: 69.3 us -> 0 us
  Pallas kernels: 0 us -> 55.6 us
  local copies, waits for them, and re-layouts: 39.4 us -> 52.7 us
    reduce_scatter x5 -> x0, waiting for transfers between devices: 177 us -> none  [the longest x4 167 us: sum_rows(): lax.psum_scatter(term_fn(jnp.int32(0), lax.axis_size('gz') * row_count).a...]
    all_gather x6 -> x0, waiting for transfers between devices: 166 us -> none  [the longest x4 162 us: gather_rows(): return lax.all_gather(tensor, 'gz', axis=0, tiled=True)]
    dot_general x96 -> x11, matrix products: 177 us -> 45.6 us  [the longest x1 6.17 us: shards(): jnp.einsum('lm,fm->lf', d_branch, down_full, preferred_element_type=F32)]
    ppermute x0 -> x54, starting transfers between devices: none -> 109 us  [the longest x2 31.3 us: sum_all(): lax.ppermute(total, 'gx', [(p, p ^ step) for p in range(planes)])]
    ppermute x0 -> x54, waiting for transfers between devices: none -> 90.4 us  [the longest x24 79.1 us: to_chip(): return lax.ppermute(value, 'gz', CHIP[k])]
    psum x2 -> x0, blocking collectives: 60 us -> none  [the longest x1 43.8 us: shards(): lax.psum((d_norm1_gain, d_norm1_bias, d_norm2_gain, d_norm2_bias, d_b_out...]
    psum x1, waiting for transfers between devices: 12.6 us -> 69.3 us  [shards(): d_w = lax.psum(d_w, 'gx').astype(F32)]
    pallas_call x0 -> x2, Pallas kernels: none -> 55.6 us  [the longest x1 29.4 us: attention_backward(): pl.pallas_call(bwd_kernel, out_shape=[S((n, 192), BF16)] * 3, in_specs=[S...]
  transfers between devices with their start and end apart: 17 -> 55, of which waited for: 14 -> 16; matrix products, arithmetic and copies ran while one was open for 23% -> 23% of each run, Pallas kernels for 0% -> 11%
where the time goes in v1:
time: 514 us; the launch traced here: 505 us
  waiting for transfers between devices  160 us (31%)
  starting transfers between devices  109 us (21%)
  other arithmetic  62.8 us (12%)
  Pallas kernels  55.6 us (11%)
  local copies, waits for them, and re-layouts  52.7 us (10%)
  matrix products  45.6 us (9%)
  between operations  18.9 us (4%)
    ppermute x24, waiting for transfers between devices, to_chip(): return lax.ppermute(value, 'gz', CHIP[k])  79.1 us
    psum x1, waiting for transfers between devices, shards(): d_w = lax.psum(d_w, 'gx').astype(F32)  69.3 us
    ppermute x2, starting transfers between devices, sum_all(): lax.ppermute(total, 'gx', [(p, p ^ step) for p in range(planes)])  31.3 us
    ppermute x24, starting transfers between devices, to_chip(): return lax.ppermute(value, 'gz', CHIP[k])  31 us
    pallas_call x1, Pallas kernels, attention_backward(): pl.pallas_call(bwd_kernel, out_shape=[S((n, 192), BF16)] * 3, in_specs=[S...  29.4 us
    pallas_call x1, Pallas kernels, attention_forward(): pl.pallas_call(fwd_kernel, out_shape=[S((n // 4, 192), BF16)] * 4 + [S((3...  26.1 us
    ppermute x12, starting transfers between devices, to_owner(): return lax.ppermute(value, CORE_CHIP, TO_OWNER[k])  21.3 us
    ppermute x12, starting transfers between devices, to_core(): return lax.ppermute(value, 'gy', CORE)  20.4 us
  transfers between devices with their start and end apart: 55, of which 16 were waited for; matrix products, arithmetic and copies ran while one was open for 23% of the time, Pallas kernels for 11%

profile of v1, /device:TPU:0, one launch (start us, length us, event | category | flops | bytes accessed | tf_op | source)
XLA Modules:
  0.0 504.6 jit_solution(1494064893141181466)
XLA Ops:
  8.0 2.0 pad_maximum_fusion.15
  10.0 3.0 collective-permute-start.17
  23.0 2.0 constant_dynamic-update-slice_fusion.8
  32.9 1.8 fusion.64
  34.7 2.1 fusion.69
  38.0 2.2 maximum_select_fusion
  44.9 2.1 pad_maximum_fusion.22
  48.8 1.7 collective-permute-start.5
  54.4 3.1 select_convert_fusion.enck
  57.4 1.8 select_convert_fusion.1.encq
  60.6 2.9 collective-permute-start.13
  67.3 1.8 collective-permute-start.1
  69.0 2.5 collective-permute-done.13
  72.0 2.0 collective-permute-start.22
  78.2 20.0 %collective-permute-done.19 = bf16[200,768]{1,0:T(8,128)(2,1)S(1)} collective-permute-done((bf16[200,768]{1,0:T(8,128)(2,1)S(1)}, bf16[200,768]{1,0:T(8,128)(2,1)S(1)}, u32[]{:S(2)}, u32[]{:S(2)}) %collective-permute-start.19) | collective-permute-done | bytes 307232 | tf_op jit(solution)/shard_map/ppermute | solution.py:285
  98.2 10.6 %collective-permute-done.18 = bf16[200,768]{1,0:T(8,128)(2,1)S(1)} collective-permute-done((bf16[200,768]{1,0:T(8,128)(2,1)S(1)}, bf16[200,768]{1,0:T(8,128)(2,1)S(1)}, u32[]{:S(2)}, u32[]{:S(2)}) %collective-permute-start.18) | collective-permute-done | bytes 307232 | tf_op jit(solution)/shard_map/ppermute | solution.py:285
  108.8 8.9 %maximum_maximum_fusion = bf16[400,3072]{1,0:T(8,128)(2,1)S(1)} fusion(bf16[200,768]{1,0:T(8,128)(2,1)S(1)} %collective-permute-done.19, bf16[200,768]{1,0:T(8,128)(2,1)S(1)} %collective-permute-done.18, bf16[400,768]{1,0:T(8,128)(2,1)S(1)} %collective-permute-done.17, bf16[400,768]{1,0:T(8,128)(2,1)S(1)} %collective-permute-done.16, ...), kind=kLoop, calls=%fused_computation.32 | loop fusion | flops 14745600 | bytes 4915200 | tf_op jit(solution)/shard_map/concatenate | solution.py:391
  120.5 1.8 collective-permute-start.24
  122.8 1.6 constant_dynamic-update-slice_fusion
  125.6 2.0 constant_dynamic-update-slice_fusion.7
  132.3 2.7 collective-permute-start.25
  136.9 26.1 %attn_fwd.1 = (bf16[512,192]{1,0:T(8,128)(2,1)S(1)}, bf16[512,192]{1,0:T(8,128)(2,1)S(1)}, bf16[512,192]{1,0:T(8,128)(2,1)S(1)}, bf16[512,192]{1,0:T(8,128)(2,1)...) custom-call(s32[3,8]{1,0:T(4,128)S(1)} %add_add_fusion.2.bounds, ...), custom_call_target="tpu_custom_call" | custom-call | tf_op jit(solution)/shard_map/attn_fwd/pallas_call | solution.py:208
  164.4 1.7 collective-permute-start.9
  166.1 4.7 collective-permute-done.11
  172.3 5.0 collective-permute-done.9
  177.4 2.4 fusion.91
  180.1 5.0 multiply_convert_fusion.1
  185.2 5.3 %fusion.92 = (f32[512]{0:T(512)S(1)}, f32[512,768]{1,0:T(8,128)S(1)}) fusion(f32[768]{0:T(1024)S(1)} %copy-done.47, bf16[512,3072]{1,0:T(8,128)(2,1)S(1)} %get-tuple-element.198, bf16[3072,384]{1,0:T(8,128)(2,1)} %collective-permute-done.25, bf16[3072,384]{1,0:T(8,128)(2,1)} %constant_dynamic-update-slice_fusion.4, f32[768]{0:T(1024)S(1)} %copy-done.46, ...), kind=kOutput, calls=%fused_computation.254 | convolution fusion | flops 2428108288 | bytes 11025408 | tf_op jit(solution)/shard_map/dot_general | solution.py:420
  190.9 2.6 multiply_reduce_fusion.1
  194.1 4.4 convolution_convert_fusion
  198.5 6.2 %convert_reduce_fusion = (f32[3072]{0:T(1024)S(1)}, bf16[512,3072]{1,0:T(8,128)(2,1)S(1)}) fusion(f32[512,3072]{1,0:T(8,128)S(1)} %get-tuple-element.199, f32[3072]{0:T(1024)S(1)} %bitcast.87, bf16[3072,384]{1,0:T(8,128)(2,1)} %collective-permute-done.25, bf16[3072,384]{1,0:T(8,128)(2,1)} %constant_dynamic-update-slice_fusion.4, ...), kind=kOutput, calls=%fused_computation.7 | convolution fusion | flops 2449339392 | bytes 15753216 | tf_op jit(solution)/shard_map/lm,fm->lf/dot_general | solution.py:430
  204.7 4.9 convolution_convert_fusion.1
  209.6 4.8 multiply_reduce_fusion
  216.7 3.2 collective-permute-start.26
  219.8 2.1 convolution_convert_fusion.4
  223.5 1.8 collective-permute-start.32
  225.3 2.3 collective-permute-start.33
  228.1 1.8 collective-permute-start.28
  232.0 3.2 slice.569
  235.3 1.6 slice.584
  236.9 3.2 collective-permute-done.28
  240.8 29.4 %attn_bwd.1 = (bf16[2048,192]{1,0:T(8,128)(2,1)}, bf16[2048,192]{1,0:T(8,128)(2,1)}, bf16[2048,192]{1,0:T(8,128)(2,1)}) custom-call(s32[3,8]{1,0:T(4,128)S(1)} %add_add_fusion.2.bounds, bf16[512,192]{1,0:T(8,128)(2,1)S(1)} %collective-permute-done.31.d0, bf16[512,192]{1,0:T(8,128)(2,1)S(1)} %collective-permute-done.32.d1, ...), custom_call_target="tpu_custom_call" | custom-call | tf_op jit(solution)/shard_map/attn_bwd/pallas_call | solution.py:217
  270.3 5.5 %fusion.17 = bf16[768,576]{0,1:T(8,128)(2,1)} fusion(bf16[512,768]{1,0:T(8,128)(2,1)S(1)} %copy-done.23, bf16[512,768]{1,0:T(8,128)(2,1)S(1)} %copy-done.21, bf16[512,768]{1,0:T(8,128)(2,1)S(1)} %copy-done.19, bf16[512,768]{1,0:T(8,128)(2,1)S(1)} %copy-done.17, bf16[2048,192]{1,0:T(8,128)(2,1)} %get-tuple-element.39, ...), kind=kOutput, calls=%fused_computation.55 | convolution fusion | flops 1832042496 | bytes 6389760 | tf_op jit(solution)/shard_map/lm,lc->mc/dot_general | solution.py:480
  279.9 3.1 concatenate.244
  283.1 2.3 copy.71
  285.4 2.4 collective-permute-start.38
  289.2 3.3 collective-permute-start.43
  293.3 4.0 collective-permute-done.43
  297.2 11.2 %collective-permute-start.39 = (bf16[400,576]{1,0:T(8,128)(2,1)S(1)}, bf16[400,576]{1,0:T(8,128)(2,1)S(1)}, u32[]{:S(2)}, u32[]{:S(2)}) collective-permute-start(bf16[400,576]{1,0:T(8,128)(2,1)S(1)} %slice.551), channel_id=1, source_target_pairs={{0,4},{4,0},{1,5},{5,1},{2,6},{6,2},{3,7},{7,3},{8,12},{12,8},{9,1... | collective-permute-start | bytes 1382408 | tf_op jit(solution)/shard_map/ppermute | solution.py:289
  308.4 3.9 convolution_convert_fusion.2
  312.5 23.5 %collective-permute-start.29 = (f32[8,768]{1,0:T(8,128)S(1)}, f32[8,768]{1,0:T(8,128)S(1)}, u32[]{:S(2)}, u32[]{:S(2)}) collective-permute-start(f32[8,768]{1,0:T(8,128)S(1)} %pad_maximum_fusion.24), channel_id=1, source_target_pairs={{0,8},{8,0},{16,24},{24,16},{1,9},{9,1},{17,25},{25,17},{2,10},{10... | collective-permute-start | bytes 73736 | tf_op jit(solution)/shard_map/ppermute | solution.py:337
  337.7 3.1 add_convert_fusion.1
  341.5 2.3 add_convert_fusion
  346.0 2.2 collective-permute-start.47
  348.2 8.9 %collective-permute-done.45 = bf16[2,192,768]{2,1,0:T(8,128)(2,1)S(1)} collective-permute-done((bf16[2,192,768]{2,1,0:T(8,128)(2,1)S(1)}, bf16[2,192,768]{2,1,0:T(8,128)(2,1)S(1)}, u32[]{:S(2)}, u32[]{:S(2)}) %collective-permute-start.45) | collective-permute-done | bytes 589856 | tf_op jit(solution)/shard_map/ppermute | solution.py:285
  357.2 2.2 collective-permute-start.46
  359.5 9.8 %collective-permute-done.50 = bf16[2,384,384]{2,1,0:T(8,128)(2,1)S(1)} collective-permute-done((bf16[2,384,384]{2,1,0:T(8,128)(2,1)S(1)}, bf16[2,384,384]{2,1,0:T(8,128)(2,1)S(1)}, u32[]{:S(2)}, u32[]{:S(2)}) %collective-permute-start.50) | collective-permute-done | bytes 589856 | tf_op jit(solution)/shard_map/ppermute | solution.py:285
  369.4 2.2 collective-permute-start.51
  375.1 8.6 %collective-permute-done.52 = bf16[2,384,384]{2,1,0:T(8,128)(2,1)S(1)} collective-permute-done((bf16[2,384,384]{2,1,0:T(8,128)(2,1)S(1)}, bf16[2,384,384]{2,1,0:T(8,128)(2,1)S(1)}, u32[]{:S(2)}, u32[]{:S(2)}) %collective-permute-start.52) | collective-permute-done | bytes 589856 | tf_op jit(solution)/shard_map/ppermute | solution.py:285
  383.7 7.4 %collective-permute-start.36 = (bf16[512,768]{1,0:T(8,128)(2,1)}, bf16[512,768]{1,0:T(8,128)(2,1)}, u32[]{:S(2)}, u32[]{:S(2)}) collective-permute-start(bf16[512,768]{1,0:T(8,128)(2,1)} %get-tuple-element.136), channel_id=1, source_target_pairs={{0,0},{1,1},{2,4},{3,5},{4,2},{5,3},{6,6},{7,7},{8,8},{9,9},{10,12... | collective-permute-start | bytes 2359304 | tf_op jit(solution)/shard_map/ppermute | solution.py:277
  391.2 4.5 collective-permute-done.51
  397.4 5.9 %collective-permute-done.53 = bf16[384,384]{1,0:T(8,128)(2,1)S(1)} collective-permute-done((bf16[384,384]{1,0:T(8,128)(2,1)S(1)}, bf16[384,384]{1,0:T(8,128)(2,1)S(1)}, u32[]{:S(2)}, u32[]{:S(2)}) %collective-permute-start.53) | collective-permute-done | bytes 294944 | tf_op jit(solution)/shard_map/ppermute | solution.py:285
  404.5 7.8 %collective-permute-start.30 = (f32[8,768]{1,0:T(8,128)S(1)}, f32[8,768]{1,0:T(8,128)S(1)}, u32[]{:S(2)}, u32[]{:S(2)}) collective-permute-start(f32[8,768]{1,0:T(8,128)S(1)} %fusion.97), channel_id=1, source_target_pairs={{0,16},{8,24},{16,0},{24,8},{1,17},{9,25},{17,1},{25,9},{2,18},{10... | collective-permute-start | bytes 73736 | tf_op jit(solution)/shard_map/ppermute | solution.py:337
  419.4 69.3 %all-reduce.3.cloned.1.call-done = (bf16[400,576]{1,0:T(8,128)(2,1)}, bf16[192,384]{1,0:T(8,128)(2,1)}, bf16[384,768]{1,0:T(8,128)(2,1)}, bf16[768,384]{1,0:T(8,128)(2,1)}) async-done(((bf16[400,576]{1,0:T(8,128)(2,1)}, bf16[192,384]{1,0:T(8,128)(2,1)}, bf16[384,768]{1,0:T(8,128)(2,1)}, bf16[768,384]{1,0:T(8,128)(2,1)}), (bf16[400,576]{1,0:T(8,128)(2,1)}, bf16[192,384]{1,0:T(8,128)(2,1)}, ...) | async-done | bytes 1787920 | tf_op jit(solution)/shard_map/psum | solution.py:492
  (372 shorter events, 92.3 us)
Async XLA Ops:
  7.2 481.4 %all-reduce.3.cloned.1.call-start = ((), (), s32[]{:S(2)}) async-start(), calls=%async_computation | async-start | bytes 3678208 | tf_op jit(solution)/shard_map/psum | solution.py:492
  10.0 50.6 %collective-permute-start.17 = (bf16[400,768]{1,0:T(8,128)(2,1)}, bf16[400,768]{1,0:T(8,128)(2,1)S(1)}, u32[]{:S(2)}, u32[]{:S(2)}) collective-permute-start(bf16[400,768]{1,0:T(8,128)(2,1)} %pad_maximum_fusion.15), channel_id=1, source_target_pairs={{0,2},{1,3},{2,0},{3,1},{4,6},{5,7},{6,4},{7,5},{8,10},{9,11},{10,... | collective-permute-start | bytes 1843208 | tf_op jit(solution)/shard_map/ppermute | solution.py:285
  13.1 50.5 %collective-permute-start.16 = (bf16[400,768]{1,0:T(8,128)(2,1)}, bf16[400,768]{1,0:T(8,128)(2,1)S(1)}, u32[]{:S(2)}, u32[]{:S(2)}) collective-permute-start(bf16[400,768]{1,0:T(8,128)(2,1)} %pad_maximum_fusion.15), channel_id=1, source_target_pairs={{0,1},{1,0},{2,3},{3,2},{4,5},{5,4},{6,7},{7,6},{8,9},{9,8},{10,11... | collective-permute-start | bytes 1843208 | tf_op jit(solution)/shard_map/ppermute | solution.py:285
  14.5 52.7 %collective-permute-start.12 = (bf16[192,384]{1,0:T(8,128)(2,1)}, bf16[192,384]{1,0:T(8,128)(2,1)}, u32[]{:S(2)}, u32[]{:S(2)}) collective-permute-start(bf16[192,384]{1,0:T(8,128)(2,1)} %param.30), channel_id=1, source_target_pairs={{0,1},{1,0},{2,3},{3,2},{4,5},{5,4},{6,7},{7,6},{8,9},{9,8},{10,11... | collective-permute-start | bytes 442376 | tf_op jit(solution)/shard_map/ppermute | solution.py:285
  16.4 32.4 %collective-permute-start = (s32[1,2048]{1,0:T(1,128)}, s32[1,2048]{1,0:T(1,128)S(1)}, u32[]{:S(2)}, u32[]{:S(2)}) collective-permute-start(s32[1,2048]{1,0:T(1,128)} %multiply_add_fusion.3), channel_id=1, source_target_pairs={{0,0},{1,1},{2,4},{3,5},{4,2},{5,3},{6,6},{7,7},{8,8},{9,9},{10,12... | collective-permute-start | bytes 24584 | tf_op jit(solution)/shard_map/ppermute | solution.py:277
  17.8 56.8 %collective-permute-start.21 = (bf16[768,384]{1,0:T(8,128)(2,1)}, bf16[768,384]{1,0:T(8,128)(2,1)}, u32[]{:S(2)}, u32[]{:S(2)}) collective-permute-start(bf16[768,384]{1,0:T(8,128)(2,1)} %param.36), channel_id=1, source_target_pairs={{0,1},{1,0},{2,3},{3,2},{4,5},{5,4},{6,7},{7,6},{8,9},{9,8},{10,11... | collective-permute-start | bytes 1769480 | tf_op jit(solution)/shard_map/ppermute | solution.py:285
  40.2 68.6 %copy-start.2 = (bf16[384,768]{1,0:T(8,128)(2,1)S(1)}, bf16[384,768]{1,0:T(8,128)(2,1)}, u32[]{:S(2)}) copy-start(bf16[384,768]{1,0:T(8,128)(2,1)} %param.34) | copy-start | bytes 1769476
  48.8 25.1 %collective-permute-start.5 = (bf16[400,576]{1,0:T(8,128)(2,1)}, bf16[400,576]{1,0:T(8,128)(2,1)S(1)}, u32[]{:S(2)}, u32[]{:S(2)}) collective-permute-start(bf16[400,576]{1,0:T(8,128)(2,1)} %pad_maximum_fusion.22), channel_id=1, source_target_pairs={{0,0},{1,1},{2,4},{3,5},{4,2},{5,3},{6,6},{7,7},{8,8},{9,9},{10,12... | collective-permute-start | bytes 1382408 | tf_op jit(solution)/shard_map/ppermute | solution.py:277
  60.6 10.9 %collective-permute-start.13 = (bf16[192,384]{1,0:T(8,128)(2,1)}, bf16[192,384]{1,0:T(8,128)(2,1)}, u32[]{:S(2)}, u32[]{:S(2)}) collective-permute-start(bf16[192,384]{1,0:T(8,128)(2,1)} %param.30), channel_id=1, source_target_pairs={{0,2},{1,3},{2,0},{3,1},{4,6},{5,7},{6,4},{7,5},{8,10},{9,11},{10,... | collective-permute-start | bytes 442376 | tf_op jit(solution)/shard_map/ppermute | solution.py:285
  63.5 8.4 %collective-permute-start.14 = (bf16[192,384]{1,0:T(8,128)(2,1)}, bf16[192,384]{1,0:T(8,128)(2,1)}, u32[]{:S(2)}, u32[]{:S(2)}) collective-permute-start(bf16[192,384]{1,0:T(8,128)(2,1)} %param.30), channel_id=1, source_target_pairs={{0,3},{1,2},{2,1},{3,0},{4,7},{5,6},{6,5},{7,4},{8,11},{9,10},{10,... | collective-permute-start | bytes 442376 | tf_op jit(solution)/shard_map/ppermute | solution.py:285
  67.3 55.1 %collective-permute-start.1 = (bf16[512,768]{1,0:T(8,128)(2,1)}, bf16[512,768]{1,0:T(8,128)(2,1)S(1)}, u32[]{:S(2)}, u32[]{:S(2)}) collective-permute-start(bf16[512,768]{1,0:T(8,128)(2,1)} %maximum_select_fusion), channel_id=1, source_target_pairs={{0,0},{1,1},{2,4},{3,5},{4,2},{5,3},{6,6},{7,7},{8,8},{9,9},{10,12... | collective-permute-start | bytes 2359304 | tf_op jit(solution)/shard_map/ppermute | solution.py:277
  71.5 50.8 %collective-permute-start.2 = (bf16[512,768]{1,0:T(8,128)(2,1)}, bf16[512,768]{1,0:T(8,128)(2,1)S(1)}, u32[]{:S(2)}, u32[]{:S(2)}) collective-permute-start(bf16[512,768]{1,0:T(8,128)(2,1)} %maximum_select_fusion), channel_id=1, source_target_pairs={{0,1},{1,0},{2,5},{3,4},{4,3},{5,2},{6,7},{7,6},{8,9},{9,8},{10,13... | collective-permute-start | bytes 2359304 | tf_op jit(solution)/shard_map/ppermute | solution.py:277
  72.0 46.0 %collective-permute-start.22 = (bf16[768,384]{1,0:T(8,128)(2,1)}, bf16[768,384]{1,0:T(8,128)(2,1)S(1)}, u32[]{:S(2)}, u32[]{:S(2)}) collective-permute-start(bf16[768,384]{1,0:T(8,128)(2,1)} %param.36), channel_id=1, source_target_pairs={{0,2},{1,3},{2,0},{3,1},{4,6},{5,7},{6,4},{7,5},{8,10},{9,11},{10,... | collective-permute-start | bytes 1769480 | tf_op jit(solution)/shard_map/ppermute | solution.py:285
  73.9 89.9 %copy-start = (bf16[400,576]{1,0:T(8,128)(2,1)}, bf16[400,576]{1,0:T(8,128)(2,1)S(1)}, u32[]{:S(2)}) copy-start(bf16[400,576]{1,0:T(8,128)(2,1)S(1)} %collective-permute-done.5.wa) | copy-start | bytes 1382404
  73.9 24.3 %collective-permute-start.19 = (bf16[200,768]{1,0:T(8,128)(2,1)S(1)}, bf16[200,768]{1,0:T(8,128)(2,1)S(1)}, u32[]{:S(2)}, u32[]{:S(2)}) collective-permute-start(bf16[200,768]{1,0:T(8,128)(2,1)S(1)} %slice.517), channel_id=1, source_target_pairs={{0,1},{1,0},{2,3},{3,2},{4,5},{5,4},{6,7},{7,6},{8,9},{9,8},{10,11... | collective-permute-start | bytes 921608 | tf_op jit(solution)/shard_map/ppermute | solution.py:285
  74.6 34.2 %collective-permute-start.18 = (bf16[200,768]{1,0:T(8,128)(2,1)S(1)}, bf16[200,768]{1,0:T(8,128)(2,1)S(1)}, u32[]{:S(2)}, u32[]{:S(2)}) collective-permute-start(bf16[200,768]{1,0:T(8,128)(2,1)S(1)} %slice.516), channel_id=1, source_target_pairs={{0,2},{1,3},{2,0},{3,1},{4,6},{5,7},{6,4},{7,5},{8,10},{9,11},{10,... | collective-permute-start | bytes 921608 | tf_op jit(solution)/shard_map/ppermute | solution.py:285
  98.2 22.3 %collective-permute-start.6 = (bf16[400,576]{1,0:T(8,128)(2,1)}, bf16[400,576]{1,0:T(8,128)(2,1)S(1)}, u32[]{:S(2)}, u32[]{:S(2)}) collective-permute-start(bf16[400,576]{1,0:T(8,128)(2,1)} %pad_maximum_fusion.22), channel_id=1, source_target_pairs={{0,4},{4,0},{1,5},{5,1},{2,6},{6,2},{3,7},{7,3},{8,12},{12,8},{9,1... | collective-permute-start | bytes 1382408 | tf_op jit(solution)/shard_map/ppermute | solution.py:289
  108.8 15.6 %collective-permute-start.23 = (bf16[384,384]{1,0:T(8,128)(2,1)S(1)}, bf16[384,384]{1,0:T(8,128)(2,1)S(1)}, u32[]{:S(2)}, u32[]{:S(2)}) collective-permute-start(bf16[384,384]{1,0:T(8,128)(2,1)S(1)} %slice.519), channel_id=1, source_target_pairs={{0,2},{1,3},{2,0},{3,1},{4,6},{5,7},{6,4},{7,5},{8,10},{9,11},{10,... | collective-permute-start | bytes 884744 | tf_op jit(solution)/shard_map/ppermute | solution.py:285
  117.9 62.2 %collective-permute-start.20 = (bf16[384,3072]{1,0:T(8,128)(2,1)S(1)}, bf16[384,3072]{1,0:T(8,128)(2,1)}, u32[]{:S(2)}, u32[]{:S(2)}) collective-permute-start(bf16[384,3072]{1,0:T(8,128)(2,1)S(1)} %slice.518), channel_id=1, source_target_pairs={{0,4},{4,0},{1,5},{5,1},{2,6},{6,2},{3,7},{7,3},{8,12},{12,8},{9,1... | collective-permute-start | bytes 7077896 | tf_op jit(solution)/shard_map/ppermute | solution.py:289
  120.5 9.0 %collective-permute-start.24 = (bf16[384,384]{1,0:T(8,128)(2,1)S(1)}, bf16[384,384]{1,0:T(8,128)(2,1)S(1)}, u32[]{:S(2)}, u32[]{:S(2)}) collective-permute-start(bf16[384,384]{1,0:T(8,128)(2,1)S(1)} %slice.520), channel_id=1, source_target_pairs={{0,1},{1,0},{2,3},{3,2},{4,5},{5,4},{6,7},{7,6},{8,9},{9,8},{10,11... | collective-permute-start | bytes 884744 | tf_op jit(solution)/shard_map/ppermute | solution.py:285
  122.3 12.8 %collective-permute-start.3 = (bf16[512,768]{1,0:T(8,128)(2,1)S(1)}, bf16[512,768]{1,0:T(8,128)(2,1)S(1)}, u32[]{:S(2)}, u32[]{:S(2)}) collective-permute-start(bf16[512,768]{1,0:T(8,128)(2,1)S(1)} %collective-permute-done.1.t0), channel_id=1, source_target_pairs={{0,4},{4,0},{1,5},{5,1},{2,6},{6,2},{3,7},{7,3},{8,12},{12,8},{9,1... | collective-permute-start | bytes 2359304 | tf_op jit(solution)/shard_map/ppermute | solution.py:289
  122.3 12.8 %collective-permute-start.4 = (bf16[512,768]{1,0:T(8,128)(2,1)S(1)}, bf16[512,768]{1,0:T(8,128)(2,1)S(1)}, u32[]{:S(2)}, u32[]{:S(2)}) collective-permute-start(bf16[512,768]{1,0:T(8,128)(2,1)S(1)} %collective-permute-done.2.t1), channel_id=1, source_target_pairs={{0,4},{4,0},{1,5},{5,1},{2,6},{6,2},{3,7},{7,3},{8,12},{12,8},{9,1... | collective-permute-start | bytes 2359304 | tf_op jit(solution)/shard_map/ppermute | solution.py:289
  124.4 7.9 %collective-permute-start.7 = (bf16[400,576]{1,0:T(8,128)(2,1)S(1)}, bf16[400,576]{1,0:T(8,128)(2,1)S(1)}, u32[]{:S(2)}, u32[]{:S(2)}) collective-permute-start(bf16[400,576]{1,0:T(8,128)(2,1)S(1)} %collective-permute-done.6), channel_id=1, source_target_pairs={{0,0},{1,1},{2,4},{3,5},{4,2},{5,3},{6,6},{7,7},{8,8},{9,9},{10,12... | collective-permute-start | bytes 1382408 | tf_op jit(solution)/shard_map/ppermute | solution.py:277
  129.5 34.9 %collective-permute-start.15 = (bf16[768,384]{1,0:T(8,128)(2,1)}, bf16[768,384]{1,0:T(8,128)(2,1)}, u32[]{:S(2)}, u32[]{:S(2)}) collective-permute-start(bf16[768,384]{1,0:T(8,128)(2,1)} %constant_dynamic-update-slice_fusion), channel_id=1, source_target_pairs={{0,4},{4,0},{1,5},{5,1},{2,6},{6,2},{3,7},{7,3},{8,12},{12,8},{9,1... | collective-permute-start | bytes 1769480 | tf_op jit(solution)/shard_map/ppermute | solution.py:289
  132.3 52.8 %collective-permute-start.25 = (bf16[3072,384]{1,0:T(8,128)(2,1)}, bf16[3072,384]{1,0:T(8,128)(2,1)}, u32[]{:S(2)}, u32[]{:S(2)}) collective-permute-start(bf16[3072,384]{1,0:T(8,128)(2,1)} %constant_dynamic-update-slice_fusion.4), channel_id=1, source_target_pairs={{0,4},{4,0},{1,5},{5,1},{2,6},{6,2},{3,7},{7,3},{8,12},{12,8},{9,1... | collective-permute-start | bytes 7077896 | tf_op jit(solution)/shard_map/ppermute | solution.py:289
  135.1 28.7 %copy-start.43 = (f32[384]{0:T(512)S(1)}, f32[384]{0:T(512)}, u32[]{:S(2)}) copy-start(f32[384]{0:T(512)} %get-tuple-element.195) | copy-start | bytes 4612
  163.0 7.7 %collective-permute-start.11 = (bf16[512,192]{1,0:T(8,128)(2,1)S(1)}, bf16[512,192]{1,0:T(8,128)(2,1)S(1)}, u32[]{:S(2)}, u32[]{:S(2)}) collective-permute-start(bf16[512,192]{1,0:T(8,128)(2,1)S(1)} %get-tuple-element.32), channel_id=1, source_target_pairs={{0,3},{1,2},{2,7},{3,6},{4,1},{5,0},{6,5},{7,4},{8,11},{9,10},{10,... | collective-permute-start | bytes 589832 | tf_op jit(solution)/shard_map/ppermute | solution.py:277
  163.8 8.5 %collective-permute-start.10 = (bf16[512,192]{1,0:T(8,128)(2,1)S(1)}, bf16[512,192]{1,0:T(8,128)(2,1)S(1)}, u32[]{:S(2)}, u32[]{:S(2)}) collective-permute-start(bf16[512,192]{1,0:T(8,128)(2,1)S(1)} %get-tuple-element.31), channel_id=1, source_target_pairs={{0,2},{1,3},{2,6},{3,7},{4,0},{5,1},{6,4},{7,5},{8,10},{9,11},{10,... | collective-permute-start | bytes 589832 | tf_op jit(solution)/shard_map/ppermute | solution.py:277
  164.4 12.9 %collective-permute-start.9 = (bf16[512,192]{1,0:T(8,128)(2,1)S(1)}, bf16[512,192]{1,0:T(8,128)(2,1)S(1)}, u32[]{:S(2)}, u32[]{:S(2)}) collective-permute-start(bf16[512,192]{1,0:T(8,128)(2,1)S(1)} %get-tuple-element.30), channel_id=1, source_target_pairs={{0,1},{1,0},{2,5},{3,4},{4,3},{5,2},{6,7},{7,6},{8,9},{9,8},{10,13... | collective-permute-start | bytes 589832 | tf_op jit(solution)/shard_map/ppermute | solution.py:277
  170.8 6.5 %collective-permute-start.8 = (bf16[512,192]{1,0:T(8,128)(2,1)S(1)}, bf16[512,192]{1,0:T(8,128)(2,1)S(1)}, u32[]{:S(2)}, u32[]{:S(2)}) collective-permute-start(bf16[512,192]{1,0:T(8,128)(2,1)S(1)} %get-tuple-element.29), channel_id=1, source_target_pairs={{0,0},{1,1},{2,4},{3,5},{4,2},{5,3},{6,6},{7,7},{8,8},{9,9},{10,12... | collective-permute-start | bytes 589832 | tf_op jit(solution)/shard_map/ppermute | solution.py:277
  216.7 5.3 %collective-permute-start.26 = (f32[11,768]{1,0:T(8,128)S(1)}, f32[11,768]{1,0:T(8,128)S(1)}, u32[]{:S(2)}, u32[]{:S(2)}) collective-permute-start(f32[11,768]{1,0:T(8,128)S(1)} %concatenate.235), channel_id=1, source_target_pairs={{0,4},{4,0},{1,5},{5,1},{2,6},{6,2},{3,7},{7,3},{8,12},{12,8},{9,1... | collective-permute-start | bytes 101384 | tf_op jit(solution)/shard_map/ppermute | solution.py:289
  222.0 6.0 %collective-permute-start.27 = (f32[11,768]{1,0:T(8,128)S(1)}, f32[11,768]{1,0:T(8,128)S(1)}, u32[]{:S(2)}, u32[]{:S(2)}) collective-permute-start(f32[11,768]{1,0:T(8,128)S(1)} %add.276), channel_id=1, source_target_pairs={{0,1},{1,0},{2,3},{3,2},{4,5},{5,4},{6,7},{7,6},{8,9},{9,8},{10,11... | collective-permute-start | bytes 101384 | tf_op jit(solution)/shard_map/ppermute | solution.py:285
  222.7 17.4 %collective-permute-start.31 = (bf16[512,192]{1,0:T(8,128)(2,1)S(1)}, bf16[512,192]{1,0:T(8,128)(2,1)S(1)}, u32[]{:S(2)}, u32[]{:S(2)}) collective-permute-start(bf16[512,192]{1,0:T(8,128)(2,1)S(1)} %get-tuple-element.145), channel_id=1, source_target_pairs={{0,0},{1,1},{2,4},{3,5},{4,2},{5,3},{6,6},{7,7},{8,8},{9,9},{10,12... | collective-permute-start | bytes 589832 | tf_op jit(solution)/shard_map/ppermute | solution.py:281
  223.5 17.2 %collective-permute-start.32 = (bf16[512,192]{1,0:T(8,128)(2,1)S(1)}, bf16[512,192]{1,0:T(8,128)(2,1)S(1)}, u32[]{:S(2)}, u32[]{:S(2)}) collective-permute-start(bf16[512,192]{1,0:T(8,128)(2,1)S(1)} %get-tuple-element.144), channel_id=1, source_target_pairs={{0,1},{1,0},{2,5},{3,4},{4,3},{5,2},{6,7},{7,6},{8,9},{9,8},{10,13... | collective-permute-start | bytes 589832 | tf_op jit(solution)/shard_map/ppermute | solution.py:281
  225.3 15.5 %collective-permute-start.33 = (bf16[512,192]{1,0:T(8,128)(2,1)S(1)}, bf16[512,192]{1,0:T(8,128)(2,1)S(1)}, u32[]{:S(2)}, u32[]{:S(2)}) collective-permute-start(bf16[512,192]{1,0:T(8,128)(2,1)S(1)} %get-tuple-element.143), channel_id=1, source_target_pairs={{0,4},{1,5},{2,0},{3,1},{4,6},{5,7},{6,2},{7,3},{8,12},{9,13},{10,... | collective-permute-start | bytes 589832 | tf_op jit(solution)/shard_map/ppermute | solution.py:281
  227.6 13.2 %collective-permute-start.34 = (bf16[512,192]{1,0:T(8,128)(2,1)S(1)}, bf16[512,192]{1,0:T(8,128)(2,1)S(1)}, u32[]{:S(2)}, u32[]{:S(2)}) collective-permute-start(bf16[512,192]{1,0:T(8,128)(2,1)S(1)} %get-tuple-element.142), channel_id=1, source_target_pairs={{0,5},{1,4},{2,1},{3,0},{4,7},{5,6},{6,3},{7,2},{8,13},{9,12},{10,... | collective-permute-start | bytes 589832 | tf_op jit(solution)/shard_map/ppermute | solution.py:281
  228.1 12.0 %collective-permute-start.28 = (f32[11,768]{1,0:T(8,128)S(1)}, f32[11,768]{1,0:T(8,128)S(1)}, u32[]{:S(2)}, u32[]{:S(2)}) collective-permute-start(f32[11,768]{1,0:T(8,128)S(1)} %pad_maximum_fusion.23), channel_id=1, source_target_pairs={{0,2},{1,3},{2,0},{3,1},{4,6},{5,7},{6,4},{7,5},{8,10},{9,11},{10,... | collective-permute-start | bytes 101384 | tf_op jit(solution)/shard_map/ppermute | solution.py:285
  240.1 47.7 %collective-permute-start.40 = (bf16[768,384]{1,0:T(8,128)(2,1)}, bf16[768,384]{1,0:T(8,128)(2,1)}, u32[]{:S(2)}, u32[]{:S(2)}) collective-permute-start(bf16[768,384]{1,0:T(8,128)(2,1)} %slice.560), channel_id=1, source_target_pairs={{0,4},{4,0},{1,5},{5,1},{2,6},{6,2},{3,7},{7,3},{8,12},{12,8},{9,1... | collective-permute-start | bytes 1769480 | tf_op jit(solution)/shard_map/ppermute | solution.py:289
  240.1 97.5 %collective-permute-start.44 = (bf16[384,3072]{1,0:T(8,128)(2,1)}, bf16[384,3072]{1,0:T(8,128)(2,1)}, u32[]{:S(2)}, u32[]{:S(2)}) collective-permute-start(bf16[384,3072]{1,0:T(8,128)(2,1)} %slice.569), channel_id=1, source_target_pairs={{0,4},{4,0},{1,5},{5,1},{2,6},{6,2},{3,7},{7,3},{8,12},{12,8},{9,1... | collective-permute-start | bytes 7077896 | tf_op jit(solution)/shard_map/ppermute | solution.py:289
  240.7 100.8 %collective-permute-start.49 = (bf16[3072,384]{1,0:T(8,128)(2,1)}, bf16[3072,384]{1,0:T(8,128)(2,1)}, u32[]{:S(2)}, u32[]{:S(2)}) collective-permute-start(bf16[3072,384]{1,0:T(8,128)(2,1)} %slice.584), channel_id=1, source_target_pairs={{0,4},{4,0},{1,5},{5,1},{2,6},{6,2},{3,7},{7,3},{8,12},{12,8},{9,1... | collective-permute-start | bytes 7077896 | tf_op jit(solution)/shard_map/ppermute | solution.py:289
  240.8 29.5 %copy-start.17 = (bf16[512,768]{1,0:T(8,128)(2,1)S(1)}, bf16[512,768]{1,0:T(8,128)(2,1)}, u32[]{:S(2)}) copy-start(bf16[512,768]{1,0:T(8,128)(2,1)} %copy-done.16) | copy-start | bytes 2359300
  240.8 29.5 %copy-start.19 = (bf16[512,768]{1,0:T(8,128)(2,1)S(1)}, bf16[512,768]{1,0:T(8,128)(2,1)}, u32[]{:S(2)}) copy-start(bf16[512,768]{1,0:T(8,128)(2,1)} %copy-done.18) | copy-start | bytes 2359300
  240.8 29.5 %copy-start.21 = (bf16[512,768]{1,0:T(8,128)(2,1)S(1)}, bf16[512,768]{1,0:T(8,128)(2,1)}, u32[]{:S(2)}) copy-start(bf16[512,768]{1,0:T(8,128)(2,1)} %copy-done.20) | copy-start | bytes 2359300
  240.8 29.5 %copy-start.23 = (bf16[512,768]{1,0:T(8,128)(2,1)S(1)}, bf16[512,768]{1,0:T(8,128)(2,1)}, u32[]{:S(2)}) copy-start(bf16[512,768]{1,0:T(8,128)(2,1)} %copy-done.22) | copy-start | bytes 2359300
  285.4 7.2 %collective-permute-start.38 = (bf16[800,576]{1,0:T(8,128)(2,1)}, bf16[800,576]{1,0:T(8,128)(2,1)S(1)}, u32[]{:S(2)}, u32[]{:S(2)}) collective-permute-start(bf16[800,576]{1,0:T(8,128)(2,1)} %copy.71), channel_id=1, source_target_pairs={{0,0},{1,1},{2,4},{3,5},{4,2},{5,3},{6,6},{7,7},{8,8},{9,9},{10,12... | collective-permute-start | bytes 2764808 | tf_op jit(solution)/shard_map/ppermute | solution.py:277
  289.2 8.0 %collective-permute-start.43 = (bf16[192,384]{1,0:T(8,128)(2,1)S(1)}, bf16[192,384]{1,0:T(8,128)(2,1)S(1)}, u32[]{:S(2)}, u32[]{:S(2)}) collective-permute-start(bf16[192,384]{1,0:T(8,128)(2,1)S(1)} %get-tuple-element.155), channel_id=1, source_target_pairs={{0,3},{1,2},{2,1},{3,0},{4,7},{5,6},{6,5},{7,4},{8,11},{9,10},{10,... | collective-permute-start | bytes 442376 | tf_op jit(solution)/shard_map/ppermute | solution.py:285
  292.6 19.9 %collective-permute-start.42 = (bf16[192,384]{1,0:T(8,128)(2,1)S(1)}, bf16[192,384]{1,0:T(8,128)(2,1)S(1)}, u32[]{:S(2)}, u32[]{:S(2)}) collective-permute-start(bf16[192,384]{1,0:T(8,128)(2,1)S(1)} %get-tuple-element.156), channel_id=1, source_target_pairs={{0,2},{1,3},{2,0},{3,1},{4,6},{5,7},{6,4},{7,5},{8,10},{9,11},{10,... | collective-permute-start | bytes 442376 | tf_op jit(solution)/shard_map/ppermute | solution.py:285
  292.6 43.3 %collective-permute-start.41 = (bf16[192,384]{1,0:T(8,128)(2,1)S(1)}, bf16[192,384]{1,0:T(8,128)(2,1)S(1)}, u32[]{:S(2)}, u32[]{:S(2)}) collective-permute-start(bf16[192,384]{1,0:T(8,128)(2,1)S(1)} %get-tuple-element.154), channel_id=1, source_target_pairs={{0,1},{1,0},{2,3},{3,2},{4,5},{5,4},{6,7},{7,6},{8,9},{9,8},{10,11... | collective-permute-start | bytes 442376 | tf_op jit(solution)/shard_map/ppermute | solution.py:285
  293.2 44.4 %slice-start.5 = ((s8[4718592]{0:T(1024)(128)(4,1)}), s8[4194304]{0:T(1024)(128)(4,1)S(1)}, s32[]{:S(2)}) async-start(s8[4718592]{0:T(1024)(128)(4,1)} %bitcast.81), calls=%async_computation.6 | async-start | bytes 8388608
  293.3 44.4 %slice-start.6 = ((s8[4718592]{0:T(1024)(128)(4,1)}), s8[524288]{0:T(1024)(128)(4,1)S(1)}, s32[]{:S(2)}) async-start(s8[4718592]{0:T(1024)(128)(4,1)} %bitcast.81), calls=%async_computation.7 | async-start | bytes 1048576
  297.2 39.5 %collective-permute-start.39 = (bf16[400,576]{1,0:T(8,128)(2,1)S(1)}, bf16[400,576]{1,0:T(8,128)(2,1)S(1)}, u32[]{:S(2)}, u32[]{:S(2)}) collective-permute-start(bf16[400,576]{1,0:T(8,128)(2,1)S(1)} %slice.551), channel_id=1, source_target_pairs={{0,4},{4,0},{1,5},{5,1},{2,6},{6,2},{3,7},{7,3},{8,12},{12,8},{9,1... | collective-permute-start | bytes 1382408 | tf_op jit(solution)/shard_map/ppermute | solution.py:289
  312.5 92.0 %collective-permute-start.29 = (f32[8,768]{1,0:T(8,128)S(1)}, f32[8,768]{1,0:T(8,128)S(1)}, u32[]{:S(2)}, u32[]{:S(2)}) collective-permute-start(f32[8,768]{1,0:T(8,128)S(1)} %pad_maximum_fusion.24), channel_id=1, source_target_pairs={{0,8},{8,0},{16,24},{24,16},{1,9},{9,1},{17,25},{25,17},{2,10},{10... | collective-permute-start | bytes 73736 | tf_op jit(solution)/shard_map/ppermute | solution.py:337
  336.0 9.6 %collective-permute-start.35 = (bf16[1024,768]{1,0:T(8,128)(2,1)S(1)}, bf16[1024,768]{1,0:T(8,128)(2,1)S(1)}, u32[]{:S(2)}, u32[]{:S(2)}) collective-permute-start(bf16[1024,768]{1,0:T(8,128)(2,1)S(1)} %slice.543), channel_id=1, source_target_pairs={{0,4},{4,0},{1,5},{5,1},{2,6},{6,2},{3,7},{7,3},{8,12},{12,8},{9,1... | collective-permute-start | bytes 4718600 | tf_op jit(solution)/shard_map/ppermute | solution.py:289
  340.9 16.2 %collective-permute-start.45 = (bf16[2,192,768]{2,1,0:T(8,128)(2,1)S(1)}, bf16[2,192,768]{2,1,0:T(8,128)(2,1)S(1)}, u32[]{:S(2)}, u32[]{:S(2)}) collective-permute-start(bf16[2,192,768]{2,1,0:T(8,128)(2,1)S(1)} %pad_maximum_fusion.16), channel_id=1, source_target_pairs={{0,1},{1,0},{2,3},{3,2},{4,5},{5,4},{6,7},{7,6},{8,9},{9,8},{10,11... | collective-permute-start | bytes 1769480 | tf_op jit(solution)/shard_map/ppermute | solution.py:285
  344.0 25.3 %collective-permute-start.50 = (bf16[2,384,384]{2,1,0:T(8,128)(2,1)S(1)}, bf16[2,384,384]{2,1,0:T(8,128)(2,1)S(1)}, u32[]{:S(2)}, u32[]{:S(2)}) collective-permute-start(bf16[2,384,384]{2,1,0:T(8,128)(2,1)S(1)} %pad_maximum_fusion.19), channel_id=1, source_target_pairs={{0,1},{1,0},{2,3},{3,2},{4,5},{5,4},{6,7},{7,6},{8,9},{9,8},{10,11... | collective-permute-start | bytes 1769480 | tf_op jit(solution)/shard_map/ppermute | solution.py:285
  346.0 25.6 %collective-permute-start.47 = (bf16[2,192,768]{2,1,0:T(8,128)(2,1)S(1)}, bf16[2,192,768]{2,1,0:T(8,128)(2,1)S(1)}, u32[]{:S(2)}, u32[]{:S(2)}) collective-permute-start(bf16[2,192,768]{2,1,0:T(8,128)(2,1)S(1)} %pad_maximum_fusion.17), channel_id=1, source_target_pairs={{0,2},{1,3},{2,0},{3,1},{4,6},{5,7},{6,4},{7,5},{8,10},{9,11},{10,... | collective-permute-start | bytes 1769480 | tf_op jit(solution)/shard_map/ppermute | solution.py:285
  357.2 14.4 %collective-permute-start.46 = (bf16[192,768]{1,0:T(8,128)(2,1)S(1)}, bf16[192,768]{1,0:T(8,128)(2,1)S(1)}, u32[]{:S(2)}, u32[]{:S(2)}) collective-permute-start(bf16[192,768]{1,0:T(8,128)(2,1)S(1)} %fusion.38), channel_id=1, source_target_pairs={{0,2},{1,3},{2,0},{3,1},{4,6},{5,7},{6,4},{7,5},{8,10},{9,11},{10,... | collective-permute-start | bytes 884744 | tf_op jit(solution)/shard_map/ppermute | solution.py:285
  359.4 24.3 %collective-permute-start.52 = (bf16[2,384,384]{2,1,0:T(8,128)(2,1)S(1)}, bf16[2,384,384]{2,1,0:T(8,128)(2,1)S(1)}, u32[]{:S(2)}, u32[]{:S(2)}) collective-permute-start(bf16[2,384,384]{2,1,0:T(8,128)(2,1)S(1)} %pad_maximum_fusion.20), channel_id=1, source_target_pairs={{0,2},{1,3},{2,0},{3,1},{4,6},{5,7},{6,4},{7,5},{8,10},{9,11},{10,... | collective-permute-start | bytes 1769480 | tf_op jit(solution)/shard_map/ppermute | solution.py:285
  369.4 26.2 %collective-permute-start.51 = (bf16[384,384]{1,0:T(8,128)(2,1)S(1)}, bf16[384,384]{1,0:T(8,128)(2,1)S(1)}, u32[]{:S(2)}, u32[]{:S(2)}) collective-permute-start(bf16[384,384]{1,0:T(8,128)(2,1)S(1)} %fusion.32), channel_id=1, source_target_pairs={{0,2},{1,3},{2,0},{3,1},{4,6},{5,7},{6,4},{7,5},{8,10},{9,11},{10,... | collective-permute-start | bytes 884744 | tf_op jit(solution)/shard_map/ppermute | solution.py:285
  371.8 24.7 %collective-permute-start.48 = (bf16[192,768]{1,0:T(8,128)(2,1)S(1)}, bf16[192,768]{1,0:T(8,128)(2,1)S(1)}, u32[]{:S(2)}, u32[]{:S(2)}) collective-permute-start(bf16[192,768]{1,0:T(8,128)(2,1)S(1)} %get-tuple-element.130), channel_id=1, source_target_pairs={{0,1},{1,0},{2,3},{3,2},{4,5},{5,4},{6,7},{7,6},{8,9},{9,8},{10,11... | collective-permute-start | bytes 884744 | tf_op jit(solution)/shard_map/ppermute | solution.py:285
  373.6 43.0 %collective-permute-start.37 = (bf16[512,768]{1,0:T(8,128)(2,1)}, bf16[512,768]{1,0:T(8,128)(2,1)}, u32[]{:S(2)}, u32[]{:S(2)}) collective-permute-start(bf16[512,768]{1,0:T(8,128)(2,1)} %get-tuple-element.137), channel_id=1, source_target_pairs={{0,1},{1,0},{2,5},{3,4},{4,3},{5,2},{6,7},{7,6},{8,9},{9,8},{10,13... | collective-permute-start | bytes 2359304 | tf_op jit(solution)/shard_map/ppermute | solution.py:277
  383.7 32.9 %collective-permute-start.36 = (bf16[512,768]{1,0:T(8,128)(2,1)}, bf16[512,768]{1,0:T(8,128)(2,1)}, u32[]{:S(2)}, u32[]{:S(2)}) collective-permute-start(bf16[512,768]{1,0:T(8,128)(2,1)} %get-tuple-element.136), channel_id=1, source_target_pairs={{0,0},{1,1},{2,4},{3,5},{4,2},{5,3},{6,6},{7,7},{8,8},{9,9},{10,12... | collective-permute-start | bytes 2359304 | tf_op jit(solution)/shard_map/ppermute | solution.py:277
  395.8 7.5 %collective-permute-start.53 = (bf16[384,384]{1,0:T(8,128)(2,1)S(1)}, bf16[384,384]{1,0:T(8,128)(2,1)S(1)}, u32[]{:S(2)}, u32[]{:S(2)}) collective-permute-start(bf16[384,384]{1,0:T(8,128)(2,1)S(1)} %get-tuple-element.124), channel_id=1, source_target_pairs={{0,1},{1,0},{2,3},{3,2},{4,5},{5,4},{6,7},{7,6},{8,9},{9,8},{10,11... | collective-permute-start | bytes 884744 | tf_op jit(solution)/shard_map/ppermute | solution.py:285
  404.5 9.6 %collective-permute-start.30 = (f32[8,768]{1,0:T(8,128)S(1)}, f32[8,768]{1,0:T(8,128)S(1)}, u32[]{:S(2)}, u32[]{:S(2)}) collective-permute-start(f32[8,768]{1,0:T(8,128)S(1)} %fusion.97), channel_id=1, source_target_pairs={{0,16},{8,24},{16,0},{24,8},{1,17},{9,25},{17,1},{25,9},{2,18},{10... | collective-permute-start | bytes 73736 | tf_op jit(solution)/shard_map/ppermute | solution.py:337
  (58 other events, 645.1 us)
Sparse Core Ops, SparseCore 0:
  404.5 84.1 all-reduce.2
